TPU v7x, 128 devices: a whole 4x4x4 slice. The times are simulated.
128 devices in a mesh: tm: 32 (over y, z, core), mel: 4 (over x).
Axes of the slice: x: 4, y: 4, z: 4, core: 2. Of those that a mesh axis runs over, the one named last changes fastest.
Arguments:
- act_one: bfloat16 [4096, 16384], P('tm', 'mel'), may hold values from -6 to 6
- act_two: bfloat16 [4096, 16384], P('tm', 'mel'), may hold values from -6 to 6
- act_three: bfloat16 [2048, 16384], P('tm', 'mel'), may hold values from -6 to 6
- act_four: bfloat16 [2048, 16384], P('tm', 'mel'), may hold values from -6 to 6
- target_one: bfloat16 [2048, 8192], P('tm', 'mel'), may hold values from -6 to 6
- target_two: bfloat16 [1024, 8192], P('tm', 'mel'), may hold values from -6 to 6
- kernel_one: bfloat16 [3, 3, 1, 64], replicated, may hold values from -2 to 2
- kernel_two: bfloat16 [3, 3, 64, 64], replicated, may hold values from -0.25 to 0.25
- kernel_three: bfloat16 [3, 3, 64, 128], replicated, may hold values from -0.25 to 0.25
- kernel_four: bfloat16 [3, 3, 128, 128], replicated, may hold values from -0.1875 to 0.1875
- mel_power: float32 [4096, 256], P('tm', 'mel'), may hold values from 0.05 to 20
- loudness: float32 [256], P('mel'), may hold values from 0.1 to 10
- filters: float32 [512, 256], replicated, may hold values from -0.375 to 0.375
- spec_real: float32 [4096, 512], P('tm', 'mel'), may hold values from -6 to 6
- spec_imag: float32 [4096, 512], P('tm', 'mel'), may hold values from -6 to 6
Outputs:
- wave_grad: float32 [2097152], P(('tm', 'mel'))
All inputs are finite; a program needn't handle non-finite values.
Results may differ from a plain program's by a relative error of at most 0.015.
Values may be sent and summed in bfloat16 or wider, within the bound.
No kernel may reach another device: no remote copies, remote signals or barrier semaphores. Data moves between devices by JAX's collectives and lax.ppermute only.
A program may use at most 64 MiB of HBM per device.

v0:
```python
import numpy as np
import jax
import jax.numpy as jnp
from jax import lax
from jax.experimental import pallas as pl
from jax.experimental.pallas import tpu as pltpu
from jax.sharding import PartitionSpec as P

F32 = jnp.float32
BF16 = jnp.bfloat16
C1 = 64
C2 = 128
NFFT = 1024
HOP = 512
L = 128
RC = 80
RF = 144
VMEM = pl.BlockSpec(memory_space=pltpu.VMEM)
SMEM = pl.BlockSpec(memory_space=pltpu.SMEM)
ROWS_M = 784


def lanes(index, width=L):
    return pl.ds(index * width, width)


def dot(lhs, rhs):
    return jnp.dot(lhs, rhs, preferred_element_type=F32)


def swap_halves(value):
    return pltpu.roll(value, 64, axis=1)


def lower_lanes(shape):
    return lax.broadcasted_iota(jnp.int32, shape, 1) < 64


def call(kernel, outs, scratch, args, specs=None, limit=24, flops=0, moved=1 << 20):
    return pl.pallas_call(
        kernel,
        out_shape=[jax.ShapeDtypeStruct(s, d) for s, d in outs],
        in_specs=specs or [VMEM] * len(args),
        out_specs=[VMEM] * len(outs),
        scratch_shapes=[pltpu.VMEM(s, d) for s, d in scratch],
        compiler_params=pltpu.CompilerParams(vmem_limit_bytes=limit << 20),
        cost_estimate=pl.CostEstimate(flops=flops, bytes_accessed=moved, transcendentals=0),
    )(*args)


def pack_rows_kernel(
    four_end, four_top, three_end, three_top, two_end, two_top, one_end, one_top,
    high_end, high_top, low_end, low_top, mel_end, re_end, im_end,
    end_out, top_out, tmp, end, top,
):
    end[...] = jnp.zeros_like(end)
    top[...] = jnp.zeros_like(top)
    for source, dest, first, count, row in (
        (four_end, end, 12, 4, 0),
        (three_end, end, 13, 3, 4),
        (two_end, end, 12, 4, 7),
        (one_end, end, 14, 2, 11),
        (four_top, top, 0, 4, 0),
        (three_top, top, 0, 2, 4),
        (two_top, top, 0, 2, 6),
        (one_top, top, 0, 1, 8),
    ):
        tmp[...] = source[...].astype(F32)
        dest[row : row + count, :] = tmp[first : first + count, :]
    for source, dest, first, count, row in (
        (high_end, end, 14, 2, 13),
        (low_end, end, 14, 2, 14),
        (high_top, top, 0, 2, 9),
        (low_top, top, 0, 1, 10),
    ):
        tmp[:, 0:2048] = source[...].astype(F32)
        for k in range(count):
            dest[row : row + 1, k * 2048 : (k + 1) * 2048] = tmp[first + k : first + k + 1, 0:2048]
    tmp[0:8, 0:64] = mel_end[...]
    mel = tmp[7:8, 0:64]
    head = mel.astype(BF16).astype(F32)
    end[15:16, 0:64] = head
    end[15:16, 128:192] = mel - head
    tmp[0:8, 256:384] = re_end[...]
    tmp[0:8, 384:512] = im_end[...]
    end[15:16, 256:512] = tmp[7:8, 256:512]
    end_out[...] = end[...].astype(BF16)
    top_out[...] = top[...].astype(BF16)


def pack_rows(a4, a3, a2, a1, t2, t1, mel, re, im):
    ends = {64: 3, 128: 7, 32: 1}
    args, specs = [], []
    for value in (a4, a3, a2, a1, t2, t1):
        rows, cols = value.shape
        for block in (ends[rows], 0):
            args.append(value)
            specs.append(pl.BlockSpec((16, cols), lambda i, block=block: (block, 0)))
    for value in (mel, re, im):
        args.append(value)
        specs.append(pl.BlockSpec((8, value.shape[1]), lambda i: (15, 0)))
    return pl.pallas_call(
        pack_rows_kernel,
        out_shape=[jax.ShapeDtypeStruct((16, 4096), BF16)] * 2,
        grid=(1,),
        in_specs=specs,
        out_specs=[VMEM] * 2,
        scratch_shapes=[pltpu.VMEM((16, 4096), F32)] * 3,
        compiler_params=pltpu.CompilerParams(vmem_limit_bytes=16 << 20),
    )(*args)


def halo_tiles(before, after, raw, tiles, tiles_two, tiles_one, span):
    raw[0, :, span] = before[:, span].astype(F32)
    raw[1, :, span] = after[:, span].astype(F32)
    for k, (dest, first, count, side) in enumerate(
        (
            (4, 0, 4, 0),
            (5, 4, 3, 0),
            (4, 7, 4, 0),
            (6, 11, 2, 0),
            (0, 0, 4, 1),
            (0, 4, 2, 1),
            (0, 6, 2, 1),
            (0, 8, 1, 1),
        )
    ):
        tiles[k, :, span] = jnp.zeros_like(tiles[k, :, span])
        tiles[k, dest : dest + count, span] = raw[side, first : first + count, span]


def target_tiles(before, after, raw, tiles_two, tiles_one):
    raw[0] = before[...].astype(F32)
    raw[1] = after[...].astype(F32)
    tiles_two[...] = jnp.zeros_like(tiles_two)
    tiles_one[...] = jnp.zeros_like(tiles_one)
    for k in range(2):
        half = slice(k * 2048, (k + 1) * 2048)
        tiles_two[0, 6 + k : 7 + k, :] = raw[0, 13:14, half]
        tiles_two[1, k : k + 1, :] = raw[1, 9:10, half]
        tiles_one[0, 6 + k : 7 + k, :] = raw[0, 14:15, half]
    tiles_one[1, 0:1, :] = raw[1, 10:11, 0:2048]


def padded(ref, tiles, kind, span):
    return jnp.concatenate(
        [tiles[kind, :, span], ref[:, span].astype(F32), tiles[kind + 4, :, span]], axis=0
    )


def repeat_rows_matrix():
    r = lax.broadcasted_iota(jnp.int32, (RC, 48), 0)
    x = lax.broadcasted_iota(jnp.int32, (RC, 48), 1)
    return jnp.where(x == lax.shift_right_logical(r, 1) + 4, 1.0, 0.0).astype(BF16)


def repeated_target(ref, tiles, span):
    values = jnp.concatenate([tiles[0, :, span], ref[:, span].astype(F32), tiles[1, :, span]], axis=0)
    return dot(repeat_rows_matrix(), values.astype(BF16))


def pooled_grads(first, second, target):
    both = jnp.maximum(first, 0.0) + jnp.maximum(second, 0.0)
    cells = both.reshape(RC // 8, 8, L)
    even = lax.broadcasted_iota(jnp.int32, cells.shape, 1) % 2 == 0
    other = jnp.where(even, pltpu.roll(cells, 7, axis=1), pltpu.roll(cells, 1, axis=1))
    feat = 0.25 * (cells + other).reshape(RC, L)
    diff = 0.25 * (feat - target)
    return jnp.where(first > 0, diff, 0.0), jnp.where(second > 0, diff, 0.0)


def lane_doubled(value, upper):
    swapped = swap_halves(value)
    low = lower_lanes(value.shape)
    return jnp.where(low, swapped, value) if upper else jnp.where(low, value, swapped)


def pack_columns_kernel(
    place, a4, a3, a2, a1, t2, t1, re, im, before, after,
    left_out, right_out, far_out, own_out, raw, tiles, tiles_two, tiles_one, spec, blocks,
):
    target_tiles(before, after, raw, tiles_two, tiles_one)
    for span in (slice(0, 512), slice(3584, 4096)):
        halo_tiles(before, after, raw, tiles, tiles_two, tiles_one, span)
    mel = place[0]
    spec[...] = jnp.zeros_like(spec)
    spec[8:136, 0:128] = re[...]
    spec[8:136, 128:256] = im[...]
    spec[7:8, :] = raw[0, 15:16, 256:512]
    for d in range(4):
        part = spec[7 + 32 * d : 55 + 32 * d, :]
        blocks[d, 0:48, :] = part[:, 0:128].astype(BF16)
        blocks[d, 48:96, :] = part[:, 128:256].astype(BF16)
    own_out[...] = blocks[mel]
    far_out[...] = blocks[lax.rem(mel + 2, 4)]
    left_out[688:784, :] = blocks[lax.rem(mel + 3, 4)]
    right_out[688:784, :] = blocks[lax.rem(mel + 1, 4)]
    keep_left = jnp.where(mel > 0, 1.0, 0.0).astype(F32)
    keep_right = jnp.where(mel < 3, 1.0, 0.0).astype(F32)
    for out, keep, pairs, wanted, three, edge, upper in (
        (left_out, keep_left, (0, 1), (0, 1, 2), (0, 1), 0, False),
        (right_out, keep_right, (14, 15), (29, 30, 31), (30, 31), 31, True),
    ):
        for p in pairs:
            columns = [padded(a4, tiles, 0, lanes(2 * p + k)) for k in range(2)]
            target = repeated_target(t2, tiles_two, lanes(p))
            for k, grad in enumerate(pooled_grads(*columns, target)):
                if 2 * p + k in wanted:
                    at = wanted.index(2 * p + k) * RC
                    out[at : at + RC, :] = (grad * keep).astype(BF16)
        for k, c in enumerate(three):
            at = 240 + k * RC
            out[at : at + RC, :] = (padded(a3, tiles, 1, lanes(c)) * keep).astype(BF16)
        out[400:544, :] = (padded(a2, tiles, 2, lanes(edge)) * keep).astype(BF16)
        one = padded(a1, tiles, 3, lanes(edge))
        low_target = jnp.concatenate(
            [
                tiles_one[0, :, lanes(edge // 2)],
                t1[:, lanes(edge // 2)].astype(F32),
                tiles_one[1, :, lanes(edge // 2)],
            ],
            axis=0,
        )
        low_target = jnp.concatenate([low_target, jnp.zeros((RF - RC, L), F32)], axis=0)
        swapped = swap_halves(low_target)
        low = lower_lanes((RF, L))
        joined = jnp.where(low, swapped, one) if upper else jnp.where(low, one, swapped)
        out[544:688, :] = (joined * keep).astype(BF16)


def weights_kernel(k4, k3, k2, k1, w4, w3, w2, w1):
    w4[...] = jnp.zeros_like(w4)
    w3[...] = jnp.zeros_like(w3)
    w2[...] = jnp.zeros_like(w2)
    for i in range(3):
        for b in range(4):
            row = (i * 4 + b) * L
            for a in range(2):
                j = 1 + a - b
                if -1 <= j <= 1:
                    w4[row : row + L, a * L : (a + 1) * L] = k4[i, j + 1]
            w3[row : row + L, :] = jnp.concatenate(
                [k3[i, 2 + a - b] if -1 <= 1 + a - b <= 1 else jnp.zeros((L, L), BF16) for a in range(2)], axis=1
            )
            row = (i * 4 + b) * 64
            parts = [k2[i, 2 + a - b] if -1 <= 1 + a - b <= 1 else jnp.zeros((64, L), BF16) for a in range(2)]
            w2[row : row + 64, :] = jnp.where(lower_lanes((64, L)), parts[0], parts[1])
    shape = (L, 256)
    lane = lax.broadcasted_iota(jnp.int32, shape, 1)
    parity = lax.shift_right_logical(lax.broadcasted_iota(jnp.int32, shape, 0), 6)
    column = lane - parity
    spot = lax.bitwise_and(lane, 63)

    def direct(p):
        total = jnp.zeros(shape, F32)
        for i in range(3):
            for j in (-1, 0, 1):
                hit = column == i * 64 + 2 * p + j
                fits = (2 * p + parity + j >= 0) & (2 * p + parity + j < 64)
                weight = jnp.broadcast_to(k1[:, i * 3 + j + 1 : i * 3 + j + 2], shape)
                total = jnp.where(hit & fits, weight, total)
        return total

    base = direct(1)
    for p in range(-1, 33):
        value = direct(p) if p in (-1, 0, 31, 32) else base if p == 1 else pltpu.roll(base, 2 * (p - 1), axis=1)
        w1[(p + 1) * L : (p + 2) * L, :] = value.astype(BF16)


def write_shifted(value, rows, pad, stores):
    pad[8 : 8 + rows, :] = value
    for i, store in enumerate(stores):
        store(pad[9 - i : 9 - i + rows, :].astype(BF16))


def pool_rows_matrix():
    r = lax.broadcasted_iota(jnp.int32, (RC, RF), 0)
    x = lax.broadcasted_iota(jnp.int32, (RC, RF), 1)
    return jnp.where(lax.shift_right_logical(x, 1) + 4 == r, 1.0, 0.0).astype(BF16)


def spread_rows_matrix():
    x = lax.broadcasted_iota(jnp.int32, (RF, RC), 0)
    r = lax.broadcasted_iota(jnp.int32, (RF, RC), 1)
    return jnp.where(lax.shift_right_logical(x, 1) + 4 == r, 1.0, 0.0).astype(BF16)


def pooled_low(second):
    rows = dot(pool_rows_matrix(), jnp.maximum(second, 0.0).astype(BF16))
    return 0.25 * (rows + swap_halves(rows))


def joined(parts):
    return jnp.concatenate(parts, axis=-1)


def interior_kernel(
    a4, a3, a2, a1, t2, t1, before, after, mel, loud, w4, w3, w2, w1,
    edge_g4, edge_g3, edge_g2, edge_a3, edge_a2, edge_low, edge_a1, part_out, factor_out,
    raw, tiles, tiles_two, tiles_one, even4, odd4, even3, odd3, back2, grad1, pad_c, pad_f, t2s,
):
    target_tiles(before, after, raw, tiles_two, tiles_one)
    halo_tiles(before, after, raw, tiles, tiles_two, tiles_one, slice(0, 4096))
    pad_c[...] = jnp.zeros_like(pad_c)
    pad_f[...] = jnp.zeros_like(pad_f)
    pad_f[8:136, 0:64] = mel[...]
    pad_f[7:8, 0:64] = raw[0, 15:16, 0:64] + raw[0, 15:16, 128:192]
    gain = loud[0:1, :]
    factor_out[...] = jnp.zeros_like(factor_out)
    factor_out[:, 0:64] = gain / (1.0 + gain * pad_f[0:RF, 0:64])
    t2s[...] = repeated_target(t2, tiles_two, slice(0, 2048))

    for p in range(16):
        columns = [padded(a4, tiles, 0, lanes(2 * p + k)) for k in range(2)]
        grads = pooled_grads(*columns, t2s[:, lanes(p)])
        if p in (0, 15):
            for k in range(2):
                edge_g4[(0 if p == 0 else 2) + k] = grads[k].astype(BF16)
        for k, store in enumerate((even4, odd4)):
            write_shifted(grads[k], RC, pad_c, [lambda v, i=i: store.__setitem__((i, p), v) for i in range(3)])
    lhs = joined([x for i in range(3) for x in (even4[i, 0:15], odd4[i, 0:15], even4[i, 1:16], odd4[i, 1:16])])
    out = dot(lhs.reshape(15 * RC, 1536), w4[...]).reshape(15, RC, 256)
    for q in range(15):
        for k, store in enumerate((odd3, even3)):
            c = 2 * q + 1 + k
            grad = jnp.where(padded(a3, tiles, 1, lanes(c)) > 0, out[q, :, k * L : (k + 1) * L], 0.0)
            if c in (1, 2, 29, 30):
                edge_g3[(1, 2, 29, 30).index(c)] = grad.astype(BF16)
            write_shifted(grad, RC, pad_c, [lambda v, i=i: store.__setitem__((i, q), v) for i in range(3)])
    for k, c in enumerate((0, 31)):
        edge_a3[k] = padded(a3, tiles, 1, lanes(c)).astype(BF16)
    lhs = joined([x for i in range(3) for x in (odd3[i, 0:14], even3[i, 0:14], odd3[i, 1:15], even3[i, 1:15])])
    out = dot(lhs.reshape(14 * RC, 1536), w3[...]).reshape(14, RC, 256)

    def low_loss(c, second):
        span = lanes(c // 2)
        target = jnp.concatenate([tiles_one[0, :, span], t1[:, span].astype(F32), tiles_one[1, :, span]], axis=0)
        return pooled_low(second) - lane_doubled(target, c % 2 == 1)

    for k, c in enumerate((0, 1, 30, 31)):
        second = padded(a2, tiles, 2, lanes(c))
        edge_a2[k] = second.astype(BF16)
        edge_low[k] = low_loss(c, second)
    spreading = spread_rows_matrix()
    last = None
    for c in range(2, 30):
        second = padded(a2, tiles, 2, lanes(c))
        grad = out[c // 2 - 1, :, (c % 2) * L : (c % 2 + 1) * L] + low_loss(c, second)
        wide = dot(spreading, (0.25 * grad).astype(BF16))
        fine = jnp.where(second > 0, wide, 0.0)
        if c in (2, 3, 28, 29):
            edge_g2[(2, 3, 28, 29).index(c)] = fine.astype(BF16)
        turned = swap_halves(fine)
        if last is not None:
            window = jnp.where(lower_lanes((RF, L)), last, turned)
            write_shifted(window, RF, pad_f, [lambda v, i=i: back2.__setitem__((i, c - 3), v) for i in range(3)])
        last = turned
    lhs = joined([x for i in range(3) for x in (back2[i, 0:26], back2[i, 1:27])])
    out = dot(lhs.reshape(26 * RF, 768), w2[...]).reshape(26, RF, L)
    for p in range(3, 29):
        grad = jnp.where(padded(a1, tiles, 3, lanes(p)) > 0, out[p - 3], 0.0)
        grad1[:, lanes(p - 3)] = grad.astype(BF16)
    for k, p in enumerate((0, 1, 2, 29, 30, 31)):
        edge_a1[k] = padded(a1, tiles, 3, lanes(p)).astype(BF16)
    part_out[...] = dot(grad1[...], w1[4 * L : 30 * L, :])


def edge_kernel(
    from_left, from_right, edge_g4, edge_g3, edge_g2, edge_a3, edge_a2, edge_low, edge_a1,
    part, factor, w4, w3, w2, w1, out_ref, shift4, shift3, back2, grad1, pad_c, pad_f, sums,
):
    pad_c[...] = jnp.zeros_like(pad_c)
    pad_f[...] = jnp.zeros_like(pad_f)
    zero_c = jnp.zeros((RC, L), F32)
    zero_f = jnp.zeros((RF, L), F32)

    def block(ref, at, rows):
        return ref[at : at + rows, :].astype(F32)

    def put(store, index, value, rows, pad):
        write_shifted(value, rows, pad, [lambda v, i=i: store.__setitem__((i, index), v) for i in range(3)])

    left, right = from_left, from_right
    columns = [zero_c] + [block(left, k * RC, RC) for k in range(3)] + [edge_g4[k].astype(F32) for k in range(4)]
    columns += [block(right, k * RC, RC) for k in range(3)] + [zero_c]
    for k, value in enumerate(columns):
        put(shift4, k, value, RC, pad_c)
    starts = (0, 2, 6, 8)
    lhs = jnp.concatenate(
        [joined([shift4[i, s + b] for i in range(3) for b in range(4)]) for s in starts], axis=0
    )
    out = dot(lhs, w4[...])
    masks = [zero_c, block(left, 240, RC), block(left, 240 + RC, RC), edge_a3[0].astype(F32)]
    masks += [edge_a3[1].astype(F32), block(right, 240, RC), block(right, 240 + RC, RC), zero_c]
    threes = []
    for k in range(8):
        value = out[(k // 2) * RC : (k // 2 + 1) * RC, (k % 2) * L : (k % 2 + 1) * L]
        threes.append(jnp.where(masks[k] > 0, value, 0.0))
    columns = threes[0:4] + [edge_g3[k].astype(F32) for k in range(4)] + threes[4:8]
    for k, value in enumerate(columns):
        put(shift3, k, value, RC, pad_c)
    lhs = jnp.concatenate(
        [joined([shift3[i, s + b] for i in range(3) for b in range(4)]) for s in starts], axis=0
    )
    out = dot(lhs, w3[...])
    spreading = spread_rows_matrix()
    twos = []
    for k in (1, 2, 3, 4, 5, 6):
        grad = out[(k // 2) * RC : (k // 2 + 1) * RC, (k % 2) * L : (k % 2 + 1) * L]
        if k in (1, 6):
            ref = left if k == 1 else right
            second = block(ref, 400, RF)
            target = block(ref, 544, RC)
            low = pooled_low(second) - lane_doubled(target, k == 6)
        else:
            second = edge_a2[k - 2].astype(F32)
            low = edge_low[k - 2]
        wide = dot(spreading, (0.25 * (grad + low)).astype(BF16))
        twos.append(jnp.where(second > 0, wide, 0.0))
    turned = [swap_halves(x) for x in twos]
    inner = [swap_halves(edge_g2[k].astype(F32)) for k in range(4)]
    low = lower_lanes((RF, L))
    chain = [zero_f] + turned[0:3] + inner[0:2]
    windows = [jnp.where(low, chain[k], chain[k + 1]) for k in range(5)]
    chain = inner[2:4] + turned[3:6] + [zero_f]
    windows += [jnp.where(low, chain[k], chain[k + 1]) for k in range(5)]
    for k, value in enumerate(windows):
        put(back2, k, value, RF, pad_f)
    lhs = jnp.concatenate(
        [joined([back2[i, s + b] for i in range(3) for b in range(2)]) for s in (0, 1, 2, 3, 5, 6, 7, 8)], axis=0
    )
    out = dot(lhs, w2[...])
    masks = [jnp.where(low, 0.0, block(left, 544, RF))] + [edge_a1[k].astype(F32) for k in range(6)]
    masks += [jnp.where(low, block(right, 544, RF), 0.0)]
    for k in range(8):
        grad = jnp.where(masks[k] > 0, out[k * RF : (k + 1) * RF, :], 0.0)
        grad1[:, lanes(k)] = grad.astype(BF16)
    total = part[...] + dot(grad1[:, 0:512], w1[0 : 4 * L, :]) + dot(grad1[:, 512:1024], w1[30 * L : 34 * L, :])
    sums[0, 8:152, :] = total
    sums[0, 0:8, :] = jnp.zeros((8, 256), F32)
    sums[0, 152:160, :] = jnp.zeros((8, 256), F32)
    log = sums[0, 9:153, 0:128] + swap_halves(sums[0, 8:152, 0:128]) + sums[0, 7:151, 128:256]
    pad_f[8:152, :] = log * factor[...]
    for d in range(4):
        out_ref[d] = pad_f[15 + 32 * d : 55 + 32 * d, 0:64]


def synthesis_kernel(place, grads, own, left, right, far, filters, table, window, out_ref, pieces, spec_re, spec_im):
    mel = place[0]
    power = jnp.zeros((40, HOP), F32)
    for j in range(4):
        power = power + dot(grads[j].astype(BF16), filters[64 * j : 64 * (j + 1), :])
    for ref, at, step in ((own, 0, 0), (left, 688, 3), (far, 0, 2), (right, 688, 1)):
        k = lax.rem(mel + step, 4)
        span = pl.ds(pl.multiple_of(k * 128, 128), 128)
        spec_re[:, span] = ref[at : at + 48, :].astype(F32)
        spec_im[:, span] = ref[at + 48 : at + 96, :].astype(F32)
    pieces[:, 0:512] = 2.0 * power * spec_re[0:40, :]
    pieces[:, 512:1024] = 2.0 * power * spec_im[0:40, :]
    odd = lax.broadcasted_iota(jnp.int32, (32, 1024), 1) % 2 == 1
    earlier = pieces[0:32, :]
    earlier = jnp.where(odd, -earlier, earlier)
    both = jnp.concatenate([pieces[1:33, :], earlier], axis=0).astype(BF16)
    frames = dot(both, table[...])
    wave = frames[0:32] * window[0:1, :] + frames[32:64] * window[1:2, :]
    for q in range(4):
        out_ref[pl.ds(q, 32, stride=4), :] = wave[:, q * 128 : (q + 1) * 128]


def dft_constants():
    k = np.arange(512)[:, None]
    n = np.arange(512)[None, :]
    angle = (k * n % NFFT) * (2.0 * np.pi / NFFT)
    table = np.concatenate([np.cos(angle), -np.sin(angle)], axis=0).astype(np.float32)
    points = np.arange(NFFT) * (2.0 * np.pi / NFFT)
    window = (0.5 - 0.5 * np.cos(points)) * NFFT ** (-0.5)
    rows = np.zeros((8, HOP), np.float32)
    rows[0:2] = window.reshape(2, HOP)
    return jnp.asarray(table).astype(BF16), jnp.asarray(rows)


def shards(
    a1, a2, a3, a4, t1, t2, kernel_one, kernel_two, kernel_three, kernel_four,
    mel_power, loudness, filters, re, im,
):
    size = lax.axis_size("tm")
    place = lax.axis_index("mel").astype(jnp.int32).reshape(1)
    end, top = pack_rows(a4, a3, a2, a1, t2, t1, mel_power, re, im)
    before = lax.ppermute(end, "tm", [(i, i + 1) for i in range(size - 1)])
    after = lax.ppermute(top, "tm", [(i + 1, i) for i in range(size - 1)])

    k4 = jnp.transpose(kernel_four, (0, 1, 3, 2))
    k3 = jnp.transpose(kernel_three, (0, 1, 3, 2))
    k3 = jnp.concatenate([k3, k3], axis=3)
    k2 = jnp.transpose(kernel_two, (0, 1, 3, 2))
    k2 = jnp.concatenate([k2, k2], axis=3)
    k1 = jnp.transpose(kernel_one.reshape(9, C1)).astype(F32)
    k1 = jnp.concatenate([k1, k1], axis=0)
    w4, w3, w2, w1 = call(
        weights_kernel,
        [((1536, 256), BF16), ((1536, 256), BF16), ((768, L), BF16), ((34 * L, 256), BF16)],
        [],
        (k4, k3, k2, k1),
        limit=8,
    )
    left_out, right_out, far_out, own = call(
        pack_columns_kernel,
        [((ROWS_M, L), BF16), ((ROWS_M, L), BF16), ((96, L), BF16), ((96, L), BF16)],
        [
            ((2, 16, 4096), F32),
            ((8, 8, 4096), F32),
            ((2, 8, 2048), F32),
            ((2, 8, 2048), F32),
            ((160, 256), F32),
            ((4, 96, L), BF16),
        ],
        (place, a4, a3, a2, a1, t2, t1, re, im, before, after),
        specs=[SMEM] + [VMEM] * 10,
        limit=12,
    )
    ring = [(i, (i + 1) % 4) for i in range(4)]
    back = [(j, i) for i, j in ring]
    from_left = lax.ppermute(right_out, "mel", ring)
    from_right = lax.ppermute(left_out, "mel", back)
    far = lax.ppermute(far_out, "mel", [(i, (i + 2) % 4) for i in range(4)])
    edges = call(
        interior_kernel,
        [
            ((4, RC, L), BF16),
            ((4, RC, L), BF16),
            ((4, RF, L), BF16),
            ((2, RC, L), BF16),
            ((4, RF, L), BF16),
            ((4, RC, L), F32),
            ((6, RF, L), BF16),
            ((RF, 256), F32),
            ((RF, L), F32),
        ],
        [
            ((2, 16, 4096), F32),
            ((8, 8, 4096), F32),
            ((2, 8, 2048), F32),
            ((2, 8, 2048), F32),
            ((3, 16, RC, L), BF16),
            ((3, 16, RC, L), BF16),
            ((3, 15, RC, L), BF16),
            ((3, 15, RC, L), BF16),
            ((3, 27, RF, L), BF16),
            ((RF, 26 * L), BF16),
            ((96, L), F32),
            ((160, L), F32),
            ((RC, 2048), F32),
        ],
        (a4, a3, a2, a1, t2, t1, before, after, mel_power, loudness.reshape(1, 64), w4, w3, w2, w1),
        limit=36,
        flops=1500000000,
    )
    (grads,) = call(
        edge_kernel,
        [((4, 40, 64), F32)],
        [
            ((3, 12, RC, L), BF16),
            ((3, 12, RC, L), BF16),
            ((3, 10, RF, L), BF16),
            ((RF, 8 * L), BF16),
            ((96, L), F32),
            ((160, L), F32),
            ((1, 160, 256), F32),
        ],
        (from_left, from_right, *edges, w4, w3, w2, w1),
        limit=16,
    )
    grads = lax.all_to_all(grads, "mel", 0, 0, tiled=True)
    table, window = dft_constants()
    turned = jnp.transpose(filters).astype(BF16)
    (wave,) = call(
        synthesis_kernel,
        [((128, 128), F32)],
        [((40, 1024), F32), ((48, 512), F32), ((48, 512), F32)],
        (place, grads, own, from_left, from_right, far, turned, table, window),
        specs=[SMEM] + [VMEM] * 8,
        limit=8,
    )
    return wave.reshape(-1)


def solution(mesh):
    return jax.shard_map(
        shards,
        mesh=mesh,
        in_specs=(
            P("tm", "mel"),
            P("tm", "mel"),
            P("tm", "mel"),
            P("tm", "mel"),
            P("tm", "mel"),
            P("tm", "mel"),
            P(),
            P(),
            P(),
            P(),
            P("tm", "mel"),
            P("mel"),
            P(),
            P("tm", "mel"),
            P("tm", "mel"),
        ),
        out_specs=P(("tm", "mel")),
        check_vma=False,
    )
```

profile of v0, /device:TPU:16, one launch (start us, length us, event | category | flops | bytes accessed | tf_op | source)
XLA Modules:
  0.0 62.2 jit_solution(7886730547764546934)
XLA Ops:
  0.0 0.8 %copy.39.mel_end.mel = f32[128,64]{1,0:T(8,128)S(1)} copy(f32[128,64]{0,1:T(8,128)} %param.27) | data formatting | bytes 65536 | tf_op args[10]
  0.9 1.2 %copy-done = bf16[128,4096]{1,0:T(8,128)(2,1)S(1)} copy-done((bf16[128,4096]{1,0:T(8,128)(2,1)S(1)}, bf16[128,4096]{1,0:T(8,128)(2,1)}, u32[]{:S(2)}) %copy-start) | copy-done | bytes 1048600
  2.1 1.2 %copy-done.2 = bf16[128,4096]{1,0:T(8,128)(2,1)S(1)} copy-done((bf16[128,4096]{1,0:T(8,128)(2,1)S(1)}, bf16[128,4096]{1,0:T(8,128)(2,1)}, u32[]{:S(2)}) %copy-start.2) | copy-done | bytes 1048600
  3.3 1.0 %copy-done.4 = bf16[64,4096]{1,0:T(8,128)(2,1)S(1)} copy-done((bf16[64,4096]{1,0:T(8,128)(2,1)S(1)}, bf16[64,4096]{1,0:T(8,128)(2,1)}, u32[]{:S(2)}) %copy-start.4) | copy-done | bytes 524312
  4.4 1.0 %copy-done.6 = bf16[64,4096]{1,0:T(8,128)(2,1)S(1)} copy-done((bf16[64,4096]{1,0:T(8,128)(2,1)S(1)}, bf16[64,4096]{1,0:T(8,128)(2,1)}, u32[]{:S(2)}) %copy-start.6) | copy-done | bytes 524312
  5.4 0.9 %copy-done.8 = bf16[64,2048]{1,0:T(8,128)(2,1)S(1)} copy-done((bf16[64,2048]{1,0:T(8,128)(2,1)S(1)}, bf16[64,2048]{1,0:T(8,128)(2,1)}, u32[]{:S(2)}) %copy-start.8) | copy-done | bytes 262168
  6.3 0.9 %copy-done.10 = bf16[32,2048]{1,0:T(8,128)(2,1)S(1)} copy-done((bf16[32,2048]{1,0:T(8,128)(2,1)S(1)}, bf16[32,2048]{1,0:T(8,128)(2,1)}, u32[]{:S(2)}) %copy-start.10) | copy-done | bytes 131096
  7.3 0.8 %copy-done.20 = f32[128,128]{1,0:T(8,128)S(1)} copy-done((f32[128,128]{1,0:T(8,128)S(1)}, f32[128,128]{1,0:T(8,128)}, u32[]{:S(2)}) %copy-start.20) | copy-done | bytes 65560
  8.1 0.8 %copy-done.22 = f32[128,128]{1,0:T(8,128)S(1)} copy-done((f32[128,128]{1,0:T(8,128)S(1)}, f32[128,128]{1,0:T(8,128)}, u32[]{:S(2)}) %copy-start.22) | copy-done | bytes 65560
  8.9 0.9 %shard_map.163 = (bf16[16,4096]{1,0:T(8,128)(2,1)}, bf16[16,4096]{1,0:T(8,128)(2,1)}) custom-call(bf16[64,4096]{1,0:T(8,128)(2,1)S(1)} %copy-done.4, bf16[64,4096]{1,0:T(8,128)(2,1)S(1)} %copy-done.4, bf16[64,4096]{1,0:T(8,128)(2,1)S(1)} %copy-done.6, bf16[64,4096]{1,0:T(8,128)(2,1)S(1)} %copy-done.6, bf16[128,4096]{1,0:T(8,128)(2,1)S(1)} %copy-done, ...), custom_call_target="tpu_custom_call" | custom-call | tf_op jit(solution)/shard_map/pallas_call | solution.py:102
  10.5 2.0 %collective-permute-start = (bf16[16,4096]{1,0:T(8,128)(2,1)}, bf16[16,4096]{1,0:T(8,128)(2,1)}, u32[]{:S(2)}, u32[]{:S(2)}) collective-permute-start(bf16[16,4096]{1,0:T(8,128)(2,1)} %get-tuple-element.24), channel_id=1, source_target_pairs={{0,4},{4,8},{8,12},{12,16},{16,20},{20,24},{24,28},{28,32},{32,36}... | collective-permute-start | bytes 393224 | tf_op jit(solution)/shard_map/ppermute | solution.py:489
  12.6 5.8 %collective-permute-start.1 = (bf16[16,4096]{1,0:T(8,128)(2,1)}, bf16[16,4096]{1,0:T(8,128)(2,1)}, u32[]{:S(2)}, u32[]{:S(2)}) collective-permute-start(bf16[16,4096]{1,0:T(8,128)(2,1)} %get-tuple-element.25), channel_id=1, source_target_pairs={{4,0},{8,4},{12,8},{16,12},{20,16},{24,20},{28,24},{32,28},{36,32}... | collective-permute-start | bytes 393224 | tf_op jit(solution)/shard_map/ppermute | solution.py:490
  18.4 1.8 %copy.41 = bf16[3,3,64,128]{2,3,1,0:T(8,128)(2,1)} copy(bf16[3,3,64,128]{3,2,1,0:T(8,128)(2,1)} %param.25) | data formatting | bytes 294912 | tf_op args[8]
  20.3 1.8 %copy.40 = bf16[3,3,128,128]{2,3,1,0:T(8,128)(2,1)} copy(bf16[3,3,128,128]{3,2,1,0:T(8,128)(2,1)} %param.26) | data formatting | bytes 589824 | tf_op args[9]
  22.1 1.7 %copy.42 = bf16[3,3,64,64]{2,3,1,0:T(8,128)(2,1)} copy(bf16[3,3,64,64]{3,2,1,0:T(8,128)(2,1)} %param.24) | data formatting | bytes 147456 | tf_op args[7]
  23.8 0.7 %copy.43.k1 = f32[128,9]{1,0:T(8,128)} copy(f32[128,9]{0,1:T(8,128)S(1)} %maximum_convert_fusion) | data formatting | bytes 9216 | tf_op jit(solution)/shard_map/concatenate | solution.py:498
  24.5 1.3 %pad_maximum_fusion.k3 = bf16[3,3,128,128]{3,2,1,0:T(8,128)(2,1)S(1)} fusion(bf16[3,3,128,64]{3,2,1,0:T(8,128)(2,1)} %bitcast.15), kind=kLoop, calls=%fused_computation | loop fusion | flops 589824 | bytes 442368 | tf_op jit(solution)/shard_map/concatenate | solution.py:494
  25.9 0.8 %copy-done.21 = f32[128,128]{1,0:T(8,128)S(1)} copy-done((f32[128,128]{1,0:T(8,128)S(1)}, f32[128,128]{1,0:T(8,128)}, u32[]{:S(2)}) %copy-start.21) | copy-done | bytes 65560
  26.7 0.8 %copy-done.23 = f32[128,128]{1,0:T(8,128)S(1)} copy-done((f32[128,128]{1,0:T(8,128)S(1)}, f32[128,128]{1,0:T(8,128)}, u32[]{:S(2)}) %copy-start.23) | copy-done | bytes 65560
  27.5 1.3 %shard_map.164 = (bf16[784,128]{1,0:T(8,128)(2,1)S(1)}, bf16[784,128]{1,0:T(8,128)(2,1)S(1)}, bf16[96,128]{1,0:T(8,128)(2,1)S(1)}, bf16[96,128]{1,0:T(8,128)(2,1)S(1)}) custom-call(s32[1]{0:T(128)} %bitcast.place, bf16[64,4096]{1,0:T(8,128)(2,1)S(1)} %copy-done.5, bf16[64,4096]{1,0:T(8,128)(2,1)S(1)} %copy-done.7, bf16[128,4096]{1,0:T(8,128)(2,1)S(1)} %copy-done.1, ...), custom_call_target="tpu_custom_call" | custom-call | bytes 1048576 | tf_op jit(solution)/shard_map/pallas_call | solution.py:40
  28.9 1.6 %collective-permute-start.2 = (bf16[784,128]{1,0:T(8,128)(2,1)S(1)}, bf16[784,128]{1,0:T(8,128)(2,1)S(1)}, u32[]{:S(2)}, u32[]{:S(2)}) collective-permute-start(bf16[784,128]{1,0:T(8,128)(2,1)S(1)} %get-tuple-element.26), channel_id=1, source_target_pairs={{0,1},{1,2},{2,3},{3,0},{4,5},{5,6},{6,7},{7,4},{8,9},{9,10},{10,1... | collective-permute-start | bytes 602120 | tf_op jit(solution)/shard_map/ppermute | solution.py:523
  30.5 1.7 %collective-permute-start.3 = (bf16[784,128]{1,0:T(8,128)(2,1)S(1)}, bf16[784,128]{1,0:T(8,128)(2,1)S(1)}, u32[]{:S(2)}, u32[]{:S(2)}) collective-permute-start(bf16[784,128]{1,0:T(8,128)(2,1)S(1)} %get-tuple-element.27), channel_id=1, source_target_pairs={{1,0},{2,1},{3,2},{0,3},{5,4},{6,5},{7,6},{4,7},{9,8},{10,9},{11,1... | collective-permute-start | bytes 602120 | tf_op jit(solution)/shard_map/ppermute | solution.py:524
  32.4 1.3 %shard_map.165 = (bf16[1536,256]{1,0:T(8,128)(2,1)S(1)}, bf16[1536,256]{1,0:T(8,128)(2,1)S(1)}, bf16[768,128]{1,0:T(8,128)(2,1)S(1)}, bf16[4352,256]{1,0:T(8,128)(2,1)S(1)}) custom-call(bf16[3,3,128,128]{3,2,1,0:T(8,128)(2,1)S(1)} %bitcast.12, bf16[3,3,128,128]{3,2,1,0:T(8,128)(2,1)S(1)} %pad_maximum_fusion.k3, ...), custom_call_target="tpu_custom_call" | custom-call | bytes 1048576 | tf_op jit(solution)/shard_map/pallas_call | solution.py:40
  33.7 10.7 %shard_map.166 = (bf16[4,80,128]{2,1,0:T(8,128)(2,1)S(1)}, bf16[4,80,128]{2,1,0:T(8,128)(2,1)S(1)}, bf16[4,144,128]{2,1,0:T(8,128)(2,1)S(1)}, bf16[2,80,128]{2,1...) custom-call(bf16[64,4096]{1,0:T(8,128)(2,1)S(1)} %copy-done.5, ...), custom_call_target="tpu_custom_call" | custom-call | flops 1500000000 | bytes 1048576 | tf_op jit(solution)/shard_map/pallas_call | solution.py:40
  44.5 2.6 %shard_map.167 = f32[4,40,64]{2,1,0:T(8,128)S(1)} custom-call(bf16[784,128]{1,0:T(8,128)(2,1)S(1)} %collective-permute-done.2.from_left.left, bf16[784,128]{1,0:T(8,128)(2,1)S(1)} %collective-permute-done.3.from_right.right, bf16[4,80,128]{2,1,0:T(8,128)(2,1)S(1)} %get-tuple-element.32.edge_g4, bf16[4,80,128]{2,1,0:T(8,128)(2,1)S(1)} %get-tuple-element.33.edge_g3, ...), custom_call_target="tpu_custom_call" | custom-call | bytes 1048576 | tf_op jit(solution)/shard_map/pallas_call | solution.py:40
  49.2 3.3 %all-to-all-start = ((f32[4,1,2560]{2,1,0:T(1,128)}), f32[4,1,2560]{2,1,0:T(1,128)S(1)}, u32[]{:S(2)}, u32[]{:S(2)}) async-start(f32[4,1,2560]{2,1,0:T(1,128)} %reshape.15), calls=%async_computation | async-start | bytes 81920 | tf_op jit(solution)/shard_map/all_to_all | solution.py:573
  52.5 3.5 %collective-permute-start.4 = (bf16[96,128]{1,0:T(8,128)(2,1)S(1)}, bf16[96,128]{1,0:T(8,128)(2,1)S(1)}, u32[]{:S(2)}, u32[]{:S(2)}) collective-permute-start(bf16[96,128]{1,0:T(8,128)(2,1)S(1)} %copy-done.30), channel_id=1, source_target_pairs={{0,2},{1,3},{2,0},{3,1},{4,6},{5,7},{6,4},{7,5},{8,10},{9,11},{10,... | collective-permute-start | bytes 73736 | tf_op jit(solution)/shard_map/ppermute | solution.py:525
  56.1 1.8 %all-to-all-done = f32[4,1,2560]{2,1,0:T(1,128)S(1)} async-done(((f32[4,1,2560]{2,1,0:T(1,128)}), f32[4,1,2560]{2,1,0:T(1,128)S(1)}, u32[]{:S(2)}, u32[]{:S(2)}) %all-to-all-start) | async-done | bytes 40992 | tf_op jit(solution)/shard_map/all_to_all | solution.py:573
  58.4 0.8 %reduce = f32[4,2560]{1,0:T(4,128)S(1)} reduce(f32[4,1,2560]{2,1,0:T(1,128)S(1)} %all-to-all-done, f32[]{:T(128)} %broadcast), dimensions={1}, to_apply=%all_to_all.3.reduce_sub_computation | reduce | bytes 81924 | tf_op jit(solution)/shard_map/all_to_all | solution.py:573
  59.3 0.9 %copy-done.15 = bf16[784,128]{1,0:T(8,128)(2,1)S(1)} copy-done((bf16[784,128]{1,0:T(8,128)(2,1)S(1)}, bf16[784,128]{1,0:T(8,128)(2,1)}, u32[]{:S(2)}) %copy-start.15) | copy-done | bytes 200728
  60.2 0.9 %copy-done.17 = bf16[784,128]{1,0:T(8,128)(2,1)S(1)} copy-done((bf16[784,128]{1,0:T(8,128)(2,1)S(1)}, bf16[784,128]{1,0:T(8,128)(2,1)}, u32[]{:S(2)}) %copy-start.17) | copy-done | bytes 200728
  61.2 1.1 %shard_map.168 = f32[128,128]{1,0:T(8,128)} custom-call(s32[1]{0:T(128)} %bitcast.place, f32[4,40,64]{2,1,0:T(8,128)S(1)} %reshape.16.grads, bf16[96,128]{1,0:T(8,128)(2,1)S(1)} %copy-done.26, bf16[784,128]{1,0:T(8,128)(2,1)S(1)} %copy-done.15, bf16[784,128]{1,0:T(8,128)(2,1)S(1)} %copy-done.17, bf16[96,128]{1,0:T(8,128)(2,1)S(1)} %collective-permute-done.4.far, ...), custom_call_target="tpu_custom_call" | custom-call | bytes 1048576 | tf_op jit(solution)/shard_map/pallas_call | solution.py:40
  (68 shorter events, 3.8 us)
Async XLA Ops:
  0.9 1.2 %copy-start = (bf16[128,4096]{1,0:T(8,128)(2,1)S(1)}, bf16[128,4096]{1,0:T(8,128)(2,1)}, u32[]{:S(2)}) copy-start(bf16[128,4096]{1,0:T(8,128)(2,1)} %a2.3) | copy-start | bytes 3145732
  2.1 1.2 %copy-start.2 = (bf16[128,4096]{1,0:T(8,128)(2,1)S(1)}, bf16[128,4096]{1,0:T(8,128)(2,1)}, u32[]{:S(2)}) copy-start(bf16[128,4096]{1,0:T(8,128)(2,1)} %a1.3) | copy-start | bytes 3145732
  3.3 1.0 %copy-start.4 = (bf16[64,4096]{1,0:T(8,128)(2,1)S(1)}, bf16[64,4096]{1,0:T(8,128)(2,1)}, u32[]{:S(2)}) copy-start(bf16[64,4096]{1,0:T(8,128)(2,1)} %a4.3) | copy-start | bytes 1572868
  4.4 1.0 %copy-start.6 = (bf16[64,4096]{1,0:T(8,128)(2,1)S(1)}, bf16[64,4096]{1,0:T(8,128)(2,1)}, u32[]{:S(2)}) copy-start(bf16[64,4096]{1,0:T(8,128)(2,1)} %a3.3) | copy-start | bytes 1572868
  5.4 0.9 %copy-start.8 = (bf16[64,2048]{1,0:T(8,128)(2,1)S(1)}, bf16[64,2048]{1,0:T(8,128)(2,1)}, u32[]{:S(2)}) copy-start(bf16[64,2048]{1,0:T(8,128)(2,1)} %t1.3) | copy-start | bytes 786436
  8.9 9.4 %copy-start.33 = (bf16[3,3,1,64]{3,1,2,0:T(4,128)(2,1)S(1)}, bf16[3,3,1,64]{3,1,2,0:T(4,128)(2,1)}, u32[]{:S(2)}) copy-start(bf16[3,3,1,64]{3,1,2,0:T(4,128)(2,1)} %param.23) | copy-start | bytes 3460
  8.9 16.9 %copy-start.3 = (bf16[128,4096]{1,0:T(8,128)(2,1)S(1)}, bf16[128,4096]{1,0:T(8,128)(2,1)}, u32[]{:S(2)}) copy-start(bf16[128,4096]{1,0:T(8,128)(2,1)} %a1.3) | copy-start | bytes 3145732
  8.9 16.9 %copy-start.7 = (bf16[64,4096]{1,0:T(8,128)(2,1)S(1)}, bf16[64,4096]{1,0:T(8,128)(2,1)}, u32[]{:S(2)}) copy-start(bf16[64,4096]{1,0:T(8,128)(2,1)} %a3.3) | copy-start | bytes 1572868
  8.9 16.9 %copy-start.9 = (bf16[64,2048]{1,0:T(8,128)(2,1)S(1)}, bf16[64,2048]{1,0:T(8,128)(2,1)}, u32[]{:S(2)}) copy-start(bf16[64,2048]{1,0:T(8,128)(2,1)} %t1.3) | copy-start | bytes 786436
  8.9 16.9 %copy-start.11 = (bf16[32,2048]{1,0:T(8,128)(2,1)S(1)}, bf16[32,2048]{1,0:T(8,128)(2,1)}, u32[]{:S(2)}) copy-start(bf16[32,2048]{1,0:T(8,128)(2,1)} %t2.3) | copy-start | bytes 393220
  10.5 15.3 %copy-start.1 = (bf16[128,4096]{1,0:T(8,128)(2,1)S(1)}, bf16[128,4096]{1,0:T(8,128)(2,1)}, u32[]{:S(2)}) copy-start(bf16[128,4096]{1,0:T(8,128)(2,1)} %a2.3) | copy-start | bytes 3145732
  10.5 15.3 %copy-start.5 = (bf16[64,4096]{1,0:T(8,128)(2,1)S(1)}, bf16[64,4096]{1,0:T(8,128)(2,1)}, u32[]{:S(2)}) copy-start(bf16[64,4096]{1,0:T(8,128)(2,1)} %a4.3) | copy-start | bytes 1572868
  10.5 15.3 %collective-permute-start = (bf16[16,4096]{1,0:T(8,128)(2,1)}, bf16[16,4096]{1,0:T(8,128)(2,1)}, u32[]{:S(2)}, u32[]{:S(2)}) collective-permute-start(bf16[16,4096]{1,0:T(8,128)(2,1)} %get-tuple-element.24), channel_id=1, source_target_pairs={{0,4},{4,8},{8,12},{12,16},{16,20},{20,24},{24,28},{28,32},{32,36}... | collective-permute-start | bytes 393224 | tf_op jit(solution)/shard_map/ppermute | solution.py:489
  12.6 13.2 %collective-permute-start.1 = (bf16[16,4096]{1,0:T(8,128)(2,1)}, bf16[16,4096]{1,0:T(8,128)(2,1)}, u32[]{:S(2)}, u32[]{:S(2)}) collective-permute-start(bf16[16,4096]{1,0:T(8,128)(2,1)} %get-tuple-element.25), channel_id=1, source_target_pairs={{4,0},{8,4},{12,8},{16,12},{20,16},{24,20},{28,24},{32,28},{36,32}... | collective-permute-start | bytes 393224 | tf_op jit(solution)/shard_map/ppermute | solution.py:490
  24.5 7.7 %copy-start.31 = (bf16[3,3,64,64]{2,3,1,0:T(8,128)(2,1)S(1)}, bf16[3,3,64,64]{2,3,1,0:T(8,128)(2,1)}, u32[]{:S(2)}) copy-start(bf16[3,3,64,64]{2,3,1,0:T(8,128)(2,1)} %copy.42) | copy-start | bytes 221188
  24.5 7.8 %copy-start.24 = (f32[128,9]{1,0:T(8,128)S(1)}, f32[128,9]{1,0:T(8,128)}, u32[]{:S(2)}) copy-start(f32[128,9]{1,0:T(8,128)} %copy.43.k1) | copy-start | bytes 13828
  25.8 6.6 %copy-start.12 = (bf16[3,3,128,128]{2,3,1,0:T(8,128)(2,1)S(1)}, bf16[3,3,128,128]{2,3,1,0:T(8,128)(2,1)}, u32[]{:S(2)}) copy-start(bf16[3,3,128,128]{2,3,1,0:T(8,128)(2,1)} %copy.40) | copy-start | bytes 884740
  27.5 6.1 %copy-start.19 = (f32[128,64]{1,0:T(8,128)S(1)}, f32[128,64]{1,0:T(8,128)}, u32[]{:S(2)}) copy-start(f32[128,64]{1,0:T(8,128)} %copy-done.18) | copy-start | bytes 98308
  27.5 6.1 %copy-start.28 = (f32[64]{0:T(128)S(1)}, f32[64]{0:T(128)}, u32[]{:S(2)}) copy-start(f32[64]{0:T(128)} %param.28) | copy-start | bytes 772
  28.9 4.7 %copy-start.25 = (bf16[96,128]{1,0:T(8,128)(2,1)}, bf16[96,128]{1,0:T(8,128)(2,1)S(1)}, u32[]{:S(2)}) copy-start(bf16[96,128]{1,0:T(8,128)(2,1)S(1)} %get-tuple-element.41.own) | copy-start | bytes 73732
  28.9 4.7 %copy-start.29 = (bf16[96,128]{1,0:T(8,128)(2,1)}, bf16[96,128]{1,0:T(8,128)(2,1)S(1)}, u32[]{:S(2)}) copy-start(bf16[96,128]{1,0:T(8,128)(2,1)S(1)} %get-tuple-element.42) | copy-start | bytes 73732
  28.9 15.5 %collective-permute-start.2 = (bf16[784,128]{1,0:T(8,128)(2,1)S(1)}, bf16[784,128]{1,0:T(8,128)(2,1)S(1)}, u32[]{:S(2)}, u32[]{:S(2)}) collective-permute-start(bf16[784,128]{1,0:T(8,128)(2,1)S(1)} %get-tuple-element.26), channel_id=1, source_target_pairs={{0,1},{1,2},{2,3},{3,0},{4,5},{5,6},{6,7},{7,4},{8,9},{9,10},{10,1... | collective-permute-start | bytes 602120 | tf_op jit(solution)/shard_map/ppermute | solution.py:523
  30.5 14.0 %collective-permute-start.3 = (bf16[784,128]{1,0:T(8,128)(2,1)S(1)}, bf16[784,128]{1,0:T(8,128)(2,1)S(1)}, u32[]{:S(2)}, u32[]{:S(2)}) collective-permute-start(bf16[784,128]{1,0:T(8,128)(2,1)S(1)} %get-tuple-element.27), channel_id=1, source_target_pairs={{1,0},{2,1},{3,2},{0,3},{5,4},{6,5},{7,6},{4,7},{9,8},{10,9},{11,1... | collective-permute-start | bytes 602120 | tf_op jit(solution)/shard_map/ppermute | solution.py:524
  44.4 8.0 %copy-start.30 = (bf16[96,128]{1,0:T(8,128)(2,1)S(1)}, bf16[96,128]{1,0:T(8,128)(2,1)}, u32[]{:S(2)}) copy-start(bf16[96,128]{1,0:T(8,128)(2,1)} %copy-done.29) | copy-start | bytes 73732
  44.4 11.5 %copy-start.32 = (f32[512,256]{1,0:T(8,128)S(1)}, f32[512,256]{1,0:T(8,128)}, u32[]{:S(2)}) copy-start(f32[512,256]{1,0:T(8,128)} %param.29) | copy-start | bytes 1572868
  44.4 14.8 %copy-start.13 = (bf16[1024,512]{1,0:T(8,128)(2,1)S(1)}, bf16[1024,512]{1,0:T(8,128)(2,1)}, u32[]{:S(2)}) copy-start(bf16[1024,512]{1,0:T(8,128)(2,1)} %constant.10.table) | copy-start | bytes 3145732
  44.5 14.8 %copy-start.26 = (bf16[96,128]{1,0:T(8,128)(2,1)S(1)}, bf16[96,128]{1,0:T(8,128)(2,1)}, u32[]{:S(2)}) copy-start(bf16[96,128]{1,0:T(8,128)(2,1)} %copy-done.25) | copy-start | bytes 73732
  44.5 14.8 %copy-start.27 = (f32[8,512]{1,0:T(8,128)S(1)}, f32[8,512]{1,0:T(8,128)}, u32[]{:S(2)}) copy-start(f32[8,512]{1,0:T(8,128)} %constant.9.clone.window) | copy-start | bytes 49156
  49.2 8.7 %all-to-all-start = ((f32[4,1,2560]{2,1,0:T(1,128)}), f32[4,1,2560]{2,1,0:T(1,128)S(1)}, u32[]{:S(2)}, u32[]{:S(2)}) async-start(f32[4,1,2560]{2,1,0:T(1,128)} %reshape.15), calls=%async_computation | async-start | bytes 81920 | tf_op jit(solution)/shard_map/all_to_all | solution.py:573
  52.5 6.8 %collective-permute-start.4 = (bf16[96,128]{1,0:T(8,128)(2,1)S(1)}, bf16[96,128]{1,0:T(8,128)(2,1)S(1)}, u32[]{:S(2)}, u32[]{:S(2)}) collective-permute-start(bf16[96,128]{1,0:T(8,128)(2,1)S(1)} %copy-done.30), channel_id=1, source_target_pairs={{0,2},{1,3},{2,0},{3,1},{4,6},{5,7},{6,4},{7,5},{8,10},{9,11},{10,... | collective-permute-start | bytes 73736 | tf_op jit(solution)/shard_map/ppermute | solution.py:525
  59.3 0.9 %copy-start.15 = (bf16[784,128]{1,0:T(8,128)(2,1)S(1)}, bf16[784,128]{1,0:T(8,128)(2,1)}, u32[]{:S(2)}) copy-start(bf16[784,128]{1,0:T(8,128)(2,1)} %copy-done.14) | copy-start | bytes 602116
  60.2 0.9 %copy-start.17 = (bf16[784,128]{1,0:T(8,128)(2,1)S(1)}, bf16[784,128]{1,0:T(8,128)(2,1)}, u32[]{:S(2)}) copy-start(bf16[784,128]{1,0:T(8,128)(2,1)} %copy-done.16) | copy-start | bytes 602116
  (8 other events, 6.2 us)
where the time goes:
time: 63.1 us; the launch traced here: 62.2 us
  local copies, waits for them, and re-layouts  22 us (35%)
  Pallas kernels  18 us (29%)
  starting transfers between devices  17.9 us (28%)
  other arithmetic  2.2 us (3%)
  waiting for transfers between devices  1.83 us (3%)
    unnamed x75, local copies, waits for them, and re-layouts  20.8 us
    pallas_call x5, Pallas kernels, call(): pl.pallas_call(kernel, out_shape=[jax.ShapeDtypeStruct(s, d) for s, d in...  17 us
    ppermute x1, starting transfers between devices, shards(): after = lax.ppermute(top, 'tm', [(i + 1, i) for i in range(size - 1)])  5.75 us
    ppermute x1, starting transfers between devices, shards(): far = lax.ppermute(far_out, 'mel', [(i, (i + 2) % 4) for i in range(4)])  3.48 us
    all_to_all x1, starting transfers between devices, shards(): grads = lax.all_to_all(grads, 'mel', 0, 0, tiled=True)  3.27 us
    ppermute x1, starting transfers between devices, shards(): before = lax.ppermute(end, 'tm', [(i, i + 1) for i in range(size - 1)])  2.04 us
    all_to_all x1, waiting for transfers between devices, shards(): grads = lax.all_to_all(grads, 'mel', 0, 0, tiled=True)  1.82 us
    ppermute x1, starting transfers between devices, shards(): from_right = lax.ppermute(left_out, 'mel', back)  1.75 us
  transfers between devices with their start and end apart: 6, of which 1 were waited for; matrix products, arithmetic and copies ran while one was open for 15% of the time, Pallas kernels for 19%

commit v1 on v0

--- a/solution.py
+++ b/solution.py
@@ -28,12 +28,20 @@
     return jnp.dot(lhs, rhs, preferred_element_type=F32)
 
 
+def dot_rows(lhs, rhs):
+    return lax.dot_general(lhs, rhs, (((1,), (1,)), ((), ())), preferred_element_type=F32)
+
+
 def swap_halves(value):
     return pltpu.roll(value, 64, axis=1)
 
 
 def lower_lanes(shape):
     return lax.broadcasted_iota(jnp.int32, shape, 1) < 64
+
+
+def pinned(*values):
+    return [pltpu.with_memory_space_constraint(value, pltpu.HBM) for value in values]
 
 
 def call(kernel, outs, scratch, args, specs=None, limit=24, flops=0, moved=1 << 20):
@@ -48,65 +56,75 @@
     )(*args)
 
 
+def fetch(copies, sems):
+    started = [pltpu.make_async_copy(s, d, sems.at[k]) for k, (s, d) in enumerate(copies)]
+    for copy in started:
+        copy.start()
+    return started
+
+
 def pack_rows_kernel(
-    four_end, four_top, three_end, three_top, two_end, two_top, one_end, one_top,
-    high_end, high_top, low_end, low_top, mel_end, re_end, im_end,
-    end_out, top_out, tmp, end, top,
+    a4, a3, a2, a1, t2, t1, re, im, mel, end_out, top_out, wide, half, mel_end, spec_end, tmp, end, top, sems
 ):
+    copies = []
+    for k, (ref, rows) in enumerate(((a4, 64), (a3, 64), (a2, 128), (a1, 128))):
+        copies += [(ref.at[rows - 16 : rows, :], wide.at[2 * k]), (ref.at[0:16, :], wide.at[2 * k + 1])]
+    for k, (ref, rows) in enumerate(((t2, 32), (t1, 64))):
+        copies += [(ref.at[rows - 16 : rows, :], half.at[2 * k]), (ref.at[0:16, :], half.at[2 * k + 1])]
+    copies += [(mel, mel_end), (re.at[120:128, :], spec_end.at[0]), (im.at[120:128, :], spec_end.at[1])]
+    started = fetch(copies, sems)
     end[...] = jnp.zeros_like(end)
     top[...] = jnp.zeros_like(top)
-    for source, dest, first, count, row in (
-        (four_end, end, 12, 4, 0),
-        (three_end, end, 13, 3, 4),
-        (two_end, end, 12, 4, 7),
-        (one_end, end, 14, 2, 11),
-        (four_top, top, 0, 4, 0),
-        (three_top, top, 0, 2, 4),
-        (two_top, top, 0, 2, 6),
-        (one_top, top, 0, 1, 8),
+    for k, (dest, first, count, row) in enumerate(
+        (
+            (end, 12, 4, 0),
+            (top, 0, 4, 0),
+            (end, 13, 3, 4),
+            (top, 0, 2, 4),
+            (end, 12, 4, 7),
+            (top, 0, 2, 6),
+            (end, 14, 2, 11),
+            (top, 0, 1, 8),
+        )
     ):
-        tmp[...] = source[...].astype(F32)
+        started[k].wait()
+        tmp[...] = wide[k].astype(F32)
         dest[row : row + count, :] = tmp[first : first + count, :]
-    for source, dest, first, count, row in (
-        (high_end, end, 14, 2, 13),
-        (low_end, end, 14, 2, 14),
-        (high_top, top, 0, 2, 9),
-        (low_top, top, 0, 1, 10),
-    ):
-        tmp[:, 0:2048] = source[...].astype(F32)
-        for k in range(count):
-            dest[row : row + 1, k * 2048 : (k + 1) * 2048] = tmp[first + k : first + k + 1, 0:2048]
-    tmp[0:8, 0:64] = mel_end[...]
-    mel = tmp[7:8, 0:64]
-    head = mel.astype(BF16).astype(F32)
+    for k, (dest, first, count, row) in enumerate(((end, 14, 2, 13), (top, 0, 2, 9), (end, 14, 2, 14), (top, 0, 1, 10))):
+        started[8 + k].wait()
+        tmp[:, 0:2048] = half[k].astype(F32)
+        for n in range(count):
+            dest[row : row + 1, n * 2048 : (n + 1) * 2048] = tmp[first + n : first + n + 1, 0:2048]
+    for copy in started[12:]:
+        copy.wait()
+    value = jnp.transpose(mel_end[...])[127:128, :]
+    head = value.astype(BF16).astype(F32)
     end[15:16, 0:64] = head
-    end[15:16, 128:192] = mel - head
-    tmp[0:8, 256:384] = re_end[...]
-    tmp[0:8, 384:512] = im_end[...]
-    end[15:16, 256:512] = tmp[7:8, 256:512]
+    end[15:16, 128:192] = value - head
+    end[15:16, 256:384] = spec_end[0, 7:8, :]
+    end[15:16, 384:512] = spec_end[1, 7:8, :]
     end_out[...] = end[...].astype(BF16)
     top_out[...] = top[...].astype(BF16)
 
 
-def pack_rows(a4, a3, a2, a1, t2, t1, mel, re, im):
-    ends = {64: 3, 128: 7, 32: 1}
-    args, specs = [], []
-    for value in (a4, a3, a2, a1, t2, t1):
-        rows, cols = value.shape
-        for block in (ends[rows], 0):
-            args.append(value)
-            specs.append(pl.BlockSpec((16, cols), lambda i, block=block: (block, 0)))
-    for value in (mel, re, im):
-        args.append(value)
-        specs.append(pl.BlockSpec((8, value.shape[1]), lambda i: (15, 0)))
+def pack_rows(*args):
     return pl.pallas_call(
         pack_rows_kernel,
         out_shape=[jax.ShapeDtypeStruct((16, 4096), BF16)] * 2,
-        grid=(1,),
-        in_specs=specs,
+        in_specs=[pl.BlockSpec(memory_space=pltpu.HBM)] * 9,
         out_specs=[VMEM] * 2,
-        scratch_shapes=[pltpu.VMEM((16, 4096), F32)] * 3,
-        compiler_params=pltpu.CompilerParams(vmem_limit_bytes=16 << 20),
+        scratch_shapes=[
+            pltpu.VMEM((8, 16, 4096), BF16),
+            pltpu.VMEM((4, 16, 2048), BF16),
+            pltpu.VMEM((64, 128), F32),
+            pltpu.VMEM((2, 8, 128), F32),
+            pltpu.VMEM((16, 4096), F32),
+            pltpu.VMEM((16, 4096), F32),
+            pltpu.VMEM((16, 4096), F32),
+            pltpu.SemaphoreType.DMA((15,)),
+        ],
+        compiler_params=pltpu.CompilerParams(vmem_limit_bytes=8 << 20),
+        cost_estimate=pl.CostEstimate(flops=0, bytes_accessed=4 << 20, transcendentals=0),
     )(*args)
 
 
@@ -148,14 +166,18 @@
     )
 
 
+def padded_edge(own, tiles, kind, span):
+    return jnp.concatenate([tiles[kind, :, span], own.astype(F32), tiles[kind + 4, :, span]], axis=0)
+
+
 def repeat_rows_matrix():
     r = lax.broadcasted_iota(jnp.int32, (RC, 48), 0)
     x = lax.broadcasted_iota(jnp.int32, (RC, 48), 1)
     return jnp.where(x == lax.shift_right_logical(r, 1) + 4, 1.0, 0.0).astype(BF16)
 
 
-def repeated_target(ref, tiles, span):
-    values = jnp.concatenate([tiles[0, :, span], ref[:, span].astype(F32), tiles[1, :, span]], axis=0)
+def repeated_target(own, tiles, span):
+    values = jnp.concatenate([tiles[0, :, span], own.astype(F32), tiles[1, :, span]], axis=0)
     return dot(repeat_rows_matrix(), values.astype(BF16))
 
 
@@ -176,7 +198,7 @@
 
 
 def pack_columns_kernel(
-    place, a4, a3, a2, a1, t2, t1, re, im, before, after,
+    place, e4, e3, e2, e1, u2, u1, own_spec, before, after,
     left_out, right_out, far_out, own_out, raw, tiles, tiles_two, tiles_one, spec, blocks,
 ):
     target_tiles(before, after, raw, tiles_two, tiles_one)
@@ -184,8 +206,8 @@
         halo_tiles(before, after, raw, tiles, tiles_two, tiles_one, span)
     mel = place[0]
     spec[...] = jnp.zeros_like(spec)
-    spec[8:136, 0:128] = re[...]
-    spec[8:136, 128:256] = im[...]
+    spec[8:136, 0:128] = own_spec[0]
+    spec[8:136, 128:256] = own_spec[1]
     spec[7:8, :] = raw[0, 15:16, 256:512]
     for d in range(4):
         part = spec[7 + 32 * d : 55 + 32 * d, :]
@@ -197,26 +219,29 @@
     right_out[688:784, :] = blocks[lax.rem(mel + 1, 4)]
     keep_left = jnp.where(mel > 0, 1.0, 0.0).astype(F32)
     keep_right = jnp.where(mel < 3, 1.0, 0.0).astype(F32)
-    for out, keep, pairs, wanted, three, edge, upper in (
+    for s, (out, keep, pairs, wanted, three, edge, upper) in enumerate((
         (left_out, keep_left, (0, 1), (0, 1, 2), (0, 1), 0, False),
         (right_out, keep_right, (14, 15), (29, 30, 31), (30, 31), 31, True),
-    ):
+    )):
         for p in pairs:
-            columns = [padded(a4, tiles, 0, lanes(2 * p + k)) for k in range(2)]
-            target = repeated_target(t2, tiles_two, lanes(p))
+            columns = [
+                padded_edge(e4[s, :, lanes((2 * p + k) % 4)], tiles, 0, lanes(2 * p + k)) for k in range(2)
+            ]
+            target = repeated_target(u2[s, :, lanes(p % 2)], tiles_two, lanes(p))
             for k, grad in enumerate(pooled_grads(*columns, target)):
                 if 2 * p + k in wanted:
                     at = wanted.index(2 * p + k) * RC
                     out[at : at + RC, :] = (grad * keep).astype(BF16)
         for k, c in enumerate(three):
             at = 240 + k * RC
-            out[at : at + RC, :] = (padded(a3, tiles, 1, lanes(c)) * keep).astype(BF16)
-        out[400:544, :] = (padded(a2, tiles, 2, lanes(edge)) * keep).astype(BF16)
-        one = padded(a1, tiles, 3, lanes(edge))
+            value = padded_edge(e3[s, :, lanes(c % 4)], tiles, 1, lanes(c))
+            out[at : at + RC, :] = (value * keep).astype(BF16)
+        out[400:544, :] = (padded_edge(e2[s, :, lanes(edge % 4)], tiles, 2, lanes(edge)) * keep).astype(BF16)
+        one = padded_edge(e1[s, :, lanes(edge % 4)], tiles, 3, lanes(edge))
         low_target = jnp.concatenate(
             [
                 tiles_one[0, :, lanes(edge // 2)],
-                t1[:, lanes(edge // 2)].astype(F32),
+                u1[s].astype(F32),
                 tiles_one[1, :, lanes(edge // 2)],
             ],
             axis=0,
@@ -228,43 +253,69 @@
         out[544:688, :] = (joined * keep).astype(BF16)
 
 
-def weights_kernel(k4, k3, k2, k1, w4, w3, w2, w1):
-    w4[...] = jnp.zeros_like(w4)
-    w3[...] = jnp.zeros_like(w3)
-    w2[...] = jnp.zeros_like(w2)
+def prepare_kernel(
+    a4, a3, a2, a1, t2, t1, re, im, k4_hbm, k3_hbm, k2_hbm, k1_hbm, filters_hbm, packed,
+    w4, w3, w2, w1, e4, e3, e2, e1, u2, u1, spec, bank, k4, k3, k2, k1, filters, sems,
+):
+    copies = [(k4_hbm, k4), (k3_hbm, k3), (k2_hbm, k2), (k1_hbm, k1), (filters_hbm, filters)]
+    for k, first in enumerate((0, 3584)):
+        for ref, dest in ((a4, e4), (a3, e3), (a2, e2), (a1, e1)):
+            copies.append((ref.at[:, first : first + 512], dest.at[k]))
+    for k in range(2):
+        copies.append((t2.at[:, k * 1792 : k * 1792 + 256], u2.at[k]))
+        copies.append((t1.at[:, k * 1920 : k * 1920 + 128], u1.at[k]))
+    copies += [(re, spec.at[0]), (im, spec.at[1])]
+    started = fetch(copies, sems)
+    for copy in started[0:4]:
+        copy.wait()
+    empty = jnp.zeros((L, L), BF16)
+    low = lower_lanes((64, L))
     for i in range(3):
         for b in range(4):
-            row = (i * 4 + b) * L
+            span = lanes(i * 4 + b)
             for a in range(2):
                 j = 1 + a - b
-                if -1 <= j <= 1:
-                    w4[row : row + L, a * L : (a + 1) * L] = k4[i, j + 1]
-            w3[row : row + L, :] = jnp.concatenate(
-                [k3[i, 2 + a - b] if -1 <= 1 + a - b <= 1 else jnp.zeros((L, L), BF16) for a in range(2)], axis=1
-            )
-            row = (i * 4 + b) * 64
-            parts = [k2[i, 2 + a - b] if -1 <= 1 + a - b <= 1 else jnp.zeros((64, L), BF16) for a in range(2)]
-            w2[row : row + 64, :] = jnp.where(lower_lanes((64, L)), parts[0], parts[1])
-    shape = (L, 256)
-    lane = lax.broadcasted_iota(jnp.int32, shape, 1)
-    parity = lax.shift_right_logical(lax.broadcasted_iota(jnp.int32, shape, 0), 6)
-    column = lane - parity
-    spot = lax.bitwise_and(lane, 63)
-
-    def direct(p):
-        total = jnp.zeros(shape, F32)
-        for i in range(3):
-            for j in (-1, 0, 1):
-                hit = column == i * 64 + 2 * p + j
-                fits = (2 * p + parity + j >= 0) & (2 * p + parity + j < 64)
-                weight = jnp.broadcast_to(k1[:, i * 3 + j + 1 : i * 3 + j + 2], shape)
-                total = jnp.where(hit & fits, weight, total)
-        return total
-
-    base = direct(1)
-    for p in range(-1, 33):
-        value = direct(p) if p in (-1, 0, 31, 32) else base if p == 1 else pltpu.roll(base, 2 * (p - 1), axis=1)
-        w1[(p + 1) * L : (p + 2) * L, :] = value.astype(BF16)
+                fits = -1 <= j <= 1
+                w4[a * L : (a + 1) * L, span] = k4[i, j + 1] if fits else empty
+                for half in range(2):
+                    row = a * L + half * 64
+                    w3[row : row + 64, span] = k3[i, j + 1] if fits else empty[0:64]
+        for b in range(0, 4, 2):
+            for a in range(2):
+                parts = []
+                for k in range(2):
+                    j = 1 + a - b - k
+                    if -1 <= j <= 1:
+                        parts.append(k2[i, j + 1].astype(F32))
+                    else:
+                        parts.append(jnp.zeros((64, 64), F32))
+                w2[a * 64 : (a + 1) * 64, lanes(i * 2 + b // 2)] = jnp.concatenate(parts, axis=1).astype(BF16)
+    w1[...] = jnp.zeros_like(w1)
+    row = lax.broadcasted_iota(jnp.int32, (16, L), 0)
+    low = lower_lanes((16, L))
+    for i in range(3):
+        taps = [jnp.concatenate([k1[i, j : j + 1, :].astype(F32)] * 2, axis=1) for j in range(3)]
+        taps = [jnp.broadcast_to(tap, (16, L)) for tap in taps]
+        zero = jnp.zeros((16, L), F32)
+        lines = [
+            jnp.where(low, taps[d] if d < 3 else zero, taps[d - 1] if d > 0 else zero) for d in range(4)
+        ]
+        tiles = {}
+        for first in (-3, -1, 1, 3, 5, 7, 9, 11, 13, 15):
+            tile = zero
+            for d in range(4):
+                tile = jnp.where(row == first + d, lines[d], tile)
+            tiles[first] = tile.astype(BF16)
+        for p in range(-1, 33):
+            for t in range(4):
+                first = 2 * p - 1 - 16 * t
+                if -4 < first < 16:
+                    at = i * 64 + t * 16
+                    w1[at : at + 16, lanes(p + 1)] = tiles[first]
+    started[4].wait()
+    bank[...] = filters[...].astype(BF16)
+    for copy in started[5:]:
+        copy.wait()
 
 
 def write_shifted(value, rows, pad, stores):
@@ -303,12 +354,12 @@
     halo_tiles(before, after, raw, tiles, tiles_two, tiles_one, slice(0, 4096))
     pad_c[...] = jnp.zeros_like(pad_c)
     pad_f[...] = jnp.zeros_like(pad_f)
-    pad_f[8:136, 0:64] = mel[...]
+    pad_f[8:136, 0:64] = jnp.transpose(mel[...])
     pad_f[7:8, 0:64] = raw[0, 15:16, 0:64] + raw[0, 15:16, 128:192]
     gain = loud[0:1, :]
     factor_out[...] = jnp.zeros_like(factor_out)
     factor_out[:, 0:64] = gain / (1.0 + gain * pad_f[0:RF, 0:64])
-    t2s[...] = repeated_target(t2, tiles_two, slice(0, 2048))
+    t2s[...] = repeated_target(t2[...], tiles_two, slice(0, 2048))
 
     for p in range(16):
         columns = [padded(a4, tiles, 0, lanes(2 * p + k)) for k in range(2)]
@@ -319,7 +370,7 @@
         for k, store in enumerate((even4, odd4)):
             write_shifted(grads[k], RC, pad_c, [lambda v, i=i: store.__setitem__((i, p), v) for i in range(3)])
     lhs = joined([x for i in range(3) for x in (even4[i, 0:15], odd4[i, 0:15], even4[i, 1:16], odd4[i, 1:16])])
-    out = dot(lhs.reshape(15 * RC, 1536), w4[...]).reshape(15, RC, 256)
+    out = dot_rows(lhs.reshape(15 * RC, 1536), w4[...]).reshape(15, RC, 256)
     for q in range(15):
         for k, store in enumerate((odd3, even3)):
             c = 2 * q + 1 + k
@@ -330,7 +381,7 @@
     for k, c in enumerate((0, 31)):
         edge_a3[k] = padded(a3, tiles, 1, lanes(c)).astype(BF16)
     lhs = joined([x for i in range(3) for x in (odd3[i, 0:14], even3[i, 0:14], odd3[i, 1:15], even3[i, 1:15])])
-    out = dot(lhs.reshape(14 * RC, 1536), w3[...]).reshape(14, RC, 256)
+    out = dot_rows(lhs.reshape(14 * RC, 1536), w3[...]).reshape(14, RC, 256)
 
     def low_loss(c, second):
         span = lanes(c // 2)
@@ -356,18 +407,19 @@
             write_shifted(window, RF, pad_f, [lambda v, i=i: back2.__setitem__((i, c - 3), v) for i in range(3)])
         last = turned
     lhs = joined([x for i in range(3) for x in (back2[i, 0:26], back2[i, 1:27])])
-    out = dot(lhs.reshape(26 * RF, 768), w2[...]).reshape(26, RF, L)
+    out = dot_rows(lhs.reshape(26 * RF, 768), w2[...]).reshape(26, RF, L)
     for p in range(3, 29):
         grad = jnp.where(padded(a1, tiles, 3, lanes(p)) > 0, out[p - 3], 0.0)
         grad1[:, lanes(p - 3)] = grad.astype(BF16)
     for k, p in enumerate((0, 1, 2, 29, 30, 31)):
         edge_a1[k] = padded(a1, tiles, 3, lanes(p)).astype(BF16)
-    part_out[...] = dot(grad1[...], w1[4 * L : 30 * L, :])
+    part_out[...] = dot_rows(grad1[...], w1[:, 4 * L : 30 * L])
 
 
 def edge_kernel(
-    from_left, from_right, edge_g4, edge_g3, edge_g2, edge_a3, edge_a2, edge_low, edge_a1,
-    part, factor, w4, w3, w2, w1, out_ref, shift4, shift3, back2, grad1, pad_c, pad_f, sums,
+    place, far_spec, from_left, from_right, edge_g4, edge_g3, edge_g2, edge_a3, edge_a2, edge_low, edge_a1,
+    part, factor, w4, w3, w2, w1, own_out, next_out, far_out, last_out,
+    shift4, shift3, back2, grad1, pad_c, pad_f, sums, blocks,
 ):
     pad_c[...] = jnp.zeros_like(pad_c)
     pad_f[...] = jnp.zeros_like(pad_f)
@@ -389,7 +441,7 @@
     lhs = jnp.concatenate(
         [joined([shift4[i, s + b] for i in range(3) for b in range(4)]) for s in starts], axis=0
     )
-    out = dot(lhs, w4[...])
+    out = dot_rows(lhs, w4[...])
     masks = [zero_c, block(left, 240, RC), block(left, 240 + RC, RC), edge_a3[0].astype(F32)]
     masks += [edge_a3[1].astype(F32), block(right, 240, RC), block(right, 240 + RC, RC), zero_c]
     threes = []
@@ -402,7 +454,7 @@
     lhs = jnp.concatenate(
         [joined([shift3[i, s + b] for i in range(3) for b in range(4)]) for s in starts], axis=0
     )
-    out = dot(lhs, w3[...])
+    out = dot_rows(lhs, w3[...])
     spreading = spread_rows_matrix()
     twos = []
     for k in (1, 2, 3, 4, 5, 6):
@@ -429,32 +481,45 @@
     lhs = jnp.concatenate(
         [joined([back2[i, s + b] for i in range(3) for b in range(2)]) for s in (0, 1, 2, 3, 5, 6, 7, 8)], axis=0
     )
-    out = dot(lhs, w2[...])
+    out = dot_rows(lhs, w2[...])
     masks = [jnp.where(low, 0.0, block(left, 544, RF))] + [edge_a1[k].astype(F32) for k in range(6)]
     masks += [jnp.where(low, block(right, 544, RF), 0.0)]
     for k in range(8):
         grad = jnp.where(masks[k] > 0, out[k * RF : (k + 1) * RF, :], 0.0)
         grad1[:, lanes(k)] = grad.astype(BF16)
-    total = part[...] + dot(grad1[:, 0:512], w1[0 : 4 * L, :]) + dot(grad1[:, 512:1024], w1[30 * L : 34 * L, :])
-    sums[0, 8:152, :] = total
-    sums[0, 0:8, :] = jnp.zeros((8, 256), F32)
-    sums[0, 152:160, :] = jnp.zeros((8, 256), F32)
-    log = sums[0, 9:153, 0:128] + swap_halves(sums[0, 8:152, 0:128]) + sums[0, 7:151, 128:256]
-    pad_f[8:152, :] = log * factor[...]
+    total = part[...] + dot_rows(grad1[:, 0:512], w1[:, 0 : 4 * L]) + dot_rows(grad1[:, 512:1024], w1[:, 30 * L : 34 * L])
+    sums[...] = jnp.zeros_like(sums)
+    sums[8:152, 0:192] = total
+    log = sums[9:153, 0:128] + swap_halves(sums[8:152, 0:128]) + sums[7:151, 128:256]
+    grad = log * factor[...]
+    mel = place[0]
+    odd = lax.rem(mel, 2) == 1
+    pad_f[8:152, :] = jnp.where(odd, swap_halves(grad), grad)
     for d in range(4):
-        out_ref[d] = pad_f[15 + 32 * d : 55 + 32 * d, 0:64]
-
-
-def synthesis_kernel(place, grads, own, left, right, far, filters, table, window, out_ref, pieces, spec_re, spec_im):
+        blocks[d] = pad_f[15 + 32 * d : 63 + 32 * d, :].astype(BF16) if d < 3 else jnp.concatenate(
+            [pad_f[111:151, :], jnp.zeros((8, L), F32)], axis=0
+        ).astype(BF16)
+    own_out[...] = blocks[mel]
+    next_out[...] = blocks[lax.rem(mel + 1, 4)]
+    last_out[...] = blocks[lax.rem(mel + 3, 4)]
+    far_out[0:48, :] = blocks[lax.rem(mel + 2, 4)]
+    far_out[48:144, :] = far_spec[...]
+
+
+def synthesis_kernel(
+    place, grad0, grad1, grad2, grad3, own, left, right, bank, table, window, out_ref, pieces, spec_re, spec_im, mels
+):
     mel = place[0]
-    power = jnp.zeros((40, HOP), F32)
-    for j in range(4):
-        power = power + dot(grads[j].astype(BF16), filters[64 * j : 64 * (j + 1), :])
-    for ref, at, step in ((own, 0, 0), (left, 688, 3), (far, 0, 2), (right, 688, 1)):
+    mels[...] = jnp.zeros_like(mels)
+    sources = ((grad0, own, 0, 0), (grad1, left, 688, 3), (grad2, grad2, 48, 2), (grad3, right, 688, 1))
+    for grad, ref, at, step in sources:
         k = lax.rem(mel + step, 4)
+        half = pl.ds(pl.multiple_of(lax.div(k, 2) * 128, 128), 128)
+        mels[:, half] = mels[:, half] + grad[0:48, :].astype(F32)
         span = pl.ds(pl.multiple_of(k * 128, 128), 128)
         spec_re[:, span] = ref[at : at + 48, :].astype(F32)
         spec_im[:, span] = ref[at + 48 : at + 96, :].astype(F32)
+    power = dot_rows(mels[...].astype(BF16), bank[...])[0:40]
     pieces[:, 0:512] = 2.0 * power * spec_re[0:40, :]
     pieces[:, 512:1024] = 2.0 * power * spec_im[0:40, :]
     odd = lax.broadcasted_iota(jnp.int32, (32, 1024), 1) % 2 == 1
@@ -485,25 +550,51 @@
 ):
     size = lax.axis_size("tm")
     place = lax.axis_index("mel").astype(jnp.int32).reshape(1)
-    end, top = pack_rows(a4, a3, a2, a1, t2, t1, mel_power, re, im)
+    mel_rows = jnp.transpose(mel_power)
+    inputs = pinned(a4, a3, a2, a1, t2, t1, re, im)
+    end, top = pack_rows(*inputs, *pinned(mel_rows))
     before = lax.ppermute(end, "tm", [(i, i + 1) for i in range(size - 1)])
     after = lax.ppermute(top, "tm", [(i + 1, i) for i in range(size - 1)])
 
-    k4 = jnp.transpose(kernel_four, (0, 1, 3, 2))
-    k3 = jnp.transpose(kernel_three, (0, 1, 3, 2))
-    k3 = jnp.concatenate([k3, k3], axis=3)
-    k2 = jnp.transpose(kernel_two, (0, 1, 3, 2))
-    k2 = jnp.concatenate([k2, k2], axis=3)
-    k1 = jnp.transpose(kernel_one.reshape(9, C1)).astype(F32)
-    k1 = jnp.concatenate([k1, k1], axis=0)
-    w4, w3, w2, w1 = call(
-        weights_kernel,
-        [((1536, 256), BF16), ((1536, 256), BF16), ((768, L), BF16), ((34 * L, 256), BF16)],
-        [],
-        (k4, k3, k2, k1),
-        limit=8,
-    )
-    left_out, right_out, far_out, own = call(
+    hbm = pl.BlockSpec(memory_space=pltpu.HBM)
+    prepared = pl.pallas_call(
+        prepare_kernel,
+        out_shape=[
+            jax.ShapeDtypeStruct(shape, kind)
+            for shape, kind in (
+                ((256, 1536), BF16),
+                ((256, 1536), BF16),
+                ((128, 768), BF16),
+                ((192, 34 * L), BF16),
+                ((2, 64, 512), BF16),
+                ((2, 64, 512), BF16),
+                ((2, 128, 512), BF16),
+                ((2, 128, 512), BF16),
+                ((2, 32, 256), BF16),
+                ((2, 64, 128), BF16),
+                ((2, 128, 128), F32),
+                ((512, 256), BF16),
+            )
+        ],
+        in_specs=[hbm] * 13 + [VMEM],
+        out_specs=[VMEM] * 12,
+        scratch_shapes=[
+            pltpu.VMEM((3, 3, 128, 128), BF16),
+            pltpu.VMEM((3, 3, 64, 128), BF16),
+            pltpu.VMEM((3, 3, 64, 64), BF16),
+            pltpu.VMEM((3, 3, 64), BF16),
+            pltpu.VMEM((512, 256), F32),
+            pltpu.SemaphoreType.DMA((19,)),
+        ],
+        compiler_params=pltpu.CompilerParams(vmem_limit_bytes=10 << 20),
+        cost_estimate=pl.CostEstimate(flops=0, bytes_accessed=8 << 20, transcendentals=0),
+    )(
+        *inputs,
+        *pinned(kernel_four, kernel_three, kernel_two, kernel_one.reshape(3, 3, C1), filters),
+        end,
+    )
+    w4, w3, w2, w1, e4, e3, e2, e1, u2, u1, spec, bank = prepared
+    left_out, right_out, far_spec, own = call(
         pack_columns_kernel,
         [((ROWS_M, L), BF16), ((ROWS_M, L), BF16), ((96, L), BF16), ((96, L), BF16)],
         [
@@ -514,15 +605,14 @@
             ((160, 256), F32),
             ((4, 96, L), BF16),
         ],
-        (place, a4, a3, a2, a1, t2, t1, re, im, before, after),
-        specs=[SMEM] + [VMEM] * 10,
-        limit=12,
+        (place, e4, e3, e2, e1, u2, u1, spec, before, after),
+        specs=[SMEM] + [VMEM] * 9,
+        limit=8,
     )
     ring = [(i, (i + 1) % 4) for i in range(4)]
     back = [(j, i) for i, j in ring]
     from_left = lax.ppermute(right_out, "mel", ring)
     from_right = lax.ppermute(left_out, "mel", back)
-    far = lax.ppermute(far_out, "mel", [(i, (i + 2) % 4) for i in range(4)])
     edges = call(
         interior_kernel,
         [
@@ -533,7 +623,7 @@
             ((4, RF, L), BF16),
             ((4, RC, L), F32),
             ((6, RF, L), BF16),
-            ((RF, 256), F32),
+            ((RF, 192), F32),
             ((RF, L), F32),
         ],
         [
@@ -551,13 +641,13 @@
             ((160, L), F32),
             ((RC, 2048), F32),
         ],
-        (a4, a3, a2, a1, t2, t1, before, after, mel_power, loudness.reshape(1, 64), w4, w3, w2, w1),
+        (a4, a3, a2, a1, t2, t1, before, after, mel_rows, loudness.reshape(1, 64), w4, w3, w2, w1),
         limit=36,
         flops=1500000000,
     )
-    (grads,) = call(
+    grad0, out1, out2, out3 = call(
         edge_kernel,
-        [((4, 40, 64), F32)],
+        [((48, L), BF16), ((48, L), BF16), ((144, L), BF16), ((48, L), BF16)],
         [
             ((3, 12, RC, L), BF16),
             ((3, 12, RC, L), BF16),
@@ -565,20 +655,23 @@
             ((RF, 8 * L), BF16),
             ((96, L), F32),
             ((160, L), F32),
-            ((1, 160, 256), F32),
+            ((160, 256), F32),
+            ((4, 48, L), BF16),
         ],
-        (from_left, from_right, *edges, w4, w3, w2, w1),
-        limit=16,
-    )
-    grads = lax.all_to_all(grads, "mel", 0, 0, tiled=True)
+        (place, far_spec, from_left, from_right, *edges, w4, w3, w2, w1),
+        specs=[SMEM] + [VMEM] * 16,
+        limit=12,
+    )
+    grad2 = lax.ppermute(out2, "mel", [(i, (i + 2) % 4) for i in range(4)])
+    grad1 = lax.ppermute(out1, "mel", ring)
+    grad3 = lax.ppermute(out3, "mel", back)
     table, window = dft_constants()
-    turned = jnp.transpose(filters).astype(BF16)
     (wave,) = call(
         synthesis_kernel,
         [((128, 128), F32)],
-        [((40, 1024), F32), ((48, 512), F32), ((48, 512), F32)],
-        (place, grads, own, from_left, from_right, far, turned, table, window),
-        specs=[SMEM] + [VMEM] * 8,
+        [((40, 1024), F32), ((48, 512), F32), ((48, 512), F32), ((48, 256), F32)],
+        (place, grad0, grad1, grad2, grad3, own, from_left, from_right, bank, table, window),
+        specs=[SMEM] + [VMEM] * 10,
         limit=8,
     )
     return wave.reshape(-1)

time: 63.1 us -> 40.7 us (0.65)
  the two profiles are of different devices: /device:TPU:16 before, /device:TPU:30 now
where the time goes in v1:
time: 40.7 us; the launch traced here: 40.5 us
  Pallas kernels  17.7 us (43%)
  starting transfers between devices  13.2 us (32%)
  waiting for transfers between devices  9.37 us (23%)
    pallas_call x4, Pallas kernels, call(): pl.pallas_call(kernel, out_shape=[jax.ShapeDtypeStruct(s, d) for s, d in...  14.2 us
    ppermute x1, starting transfers between devices, shards(): after = lax.ppermute(top, 'tm', [(i + 1, i) for i in range(size - 1)])  5.57 us
    ppermute x1, waiting for transfers between devices, shards(): before = lax.ppermute(end, 'tm', [(i, i + 1) for i in range(size - 1)])  4.45 us
    ppermute x1, waiting for transfers between devices, shards(): grad3 = lax.ppermute(out3, 'mel', back)  3.3 us
    ppermute x1, starting transfers between devices, shards(): grad1 = lax.ppermute(out1, 'mel', ring)  2.09 us
    ppermute x1, starting transfers between devices, shards(): before = lax.ppermute(end, 'tm', [(i, i + 1) for i in range(size - 1)])  1.92 us
    pallas_call x1, Pallas kernels, shards(): pl.pallas_call(prepare_kernel, out_shape=[jax.ShapeDtypeStruct(shape, kin...  1.89 us
    pallas_call x1, Pallas kernels, pack_rows(): pl.pallas_call(pack_rows_kernel, out_shape=[jax.ShapeDtypeStruct((16, 409...  1.65 us
  transfers between devices with their start and end apart: 7, of which 3 were waited for; matrix products, arithmetic and copies ran while one was open for 0% of the time, Pallas kernels for 29%

profile of v1, /device:TPU:30, one launch (start us, length us, event | category | flops | bytes accessed | tf_op | source)
XLA Modules:
  0.0 40.5 jit_solution(10195018913359558796)
XLA Ops:
  0.0 1.6 %shard_map.163 = (bf16[16,4096]{1,0:T(8,128)(2,1)S(1)}, bf16[16,4096]{1,0:T(8,128)(2,1)S(1)}) custom-call(bf16[64,4096]{1,0:T(8,128)(2,1)} %a4.5, bf16[64,4096]{1,0:T(8,128)(2,1)} %a3.5, bf16[128,4096]{1,0:T(8,128)(2,1)} %a2.5, bf16[128,4096]{1,0:T(8,128)(2,1)} %a1.5, bf16[32,2048]{1,0:T(8,128)(2,1)} %t2.5, bf16[64,2048]{1,0:T(8,128)(2,1)} %t1.5, ...), custom_call_target="tpu_custom_call" | custom-call | bytes 4194304 | tf_op jit(solution)/shard_map/pallas_call | solution.py:111
  1.7 5.6 %collective-permute-start.1 = (bf16[16,4096]{1,0:T(8,128)(2,1)S(1)}, bf16[16,4096]{1,0:T(8,128)(2,1)S(1)}, u32[]{:S(2)}, u32[]{:S(2)}) collective-permute-start(bf16[16,4096]{1,0:T(8,128)(2,1)S(1)} %get-tuple-element.44), channel_id=1, source_target_pairs={{4,0},{8,4},{12,8},{16,12},{20,16},{24,20},{28,24},{32,28},{36,32}... | collective-permute-start | bytes 393224 | tf_op jit(solution)/shard_map/ppermute | solution.py:557
  7.2 1.9 %collective-permute-start = (bf16[16,4096]{1,0:T(8,128)(2,1)S(1)}, bf16[16,4096]{1,0:T(8,128)(2,1)S(1)}, u32[]{:S(2)}, u32[]{:S(2)}) collective-permute-start(bf16[16,4096]{1,0:T(8,128)(2,1)S(1)} %get-tuple-element.36.packed), channel_id=1, source_target_pairs={{0,4},{4,8},{8,12},{12,16},{16,20},{20,24},{24,28},{28,32},{32,36}... | collective-permute-start | bytes 393224 | tf_op jit(solution)/shard_map/ppermute | solution.py:556
  9.2 0.0 copy-start.1
  9.2 0.0 copy-start.2
  9.2 0.0 copy-start.3
  9.2 0.0 copy-start.4
  9.2 0.0 copy-start.5
  9.2 0.0 copy-start.7
  9.2 0.0 copy-start.9
  9.2 1.9 %shard_map.164 = (bf16[256,1536]{1,0:T(8,128)(2,1)S(1)}, bf16[256,1536]{1,0:T(8,128)(2,1)S(1)}, bf16[128,768]{1,0:T(8,128)(2,1)S(1)}, bf16[192,4352]{1,0:T(8,128...) custom-call(bf16[64,4096]{1,0:T(8,128)(2,1)} %a4.5, ...), custom_call_target="tpu_custom_call" | custom-call | bytes 8388608 | tf_op jit(solution)/shard_map/pallas_call | solution.py:560
  11.1 0.0 copy-start
  11.2 0.0 collective-permute-done.1.after
  11.2 4.5 %collective-permute-done.before = bf16[16,4096]{1,0:T(8,128)(2,1)S(1)} collective-permute-done((bf16[16,4096]{1,0:T(8,128)(2,1)S(1)}, bf16[16,4096]{1,0:T(8,128)(2,1)S(1)}, u32[]{:S(2)}, u32[]{:S(2)}) %collective-permute-start) | collective-permute-done | bytes 131104 | tf_op jit(solution)/shard_map/ppermute | solution.py:556
  15.6 0.3 shard_map.165
  15.9 0.5 %collective-permute-start.2 = (bf16[784,128]{1,0:T(8,128)(2,1)S(1)}, bf16[784,128]{1,0:T(8,128)(2,1)S(1)}, u32[]{:S(2)}, u32[]{:S(2)}) collective-permute-start(bf16[784,128]{1,0:T(8,128)(2,1)S(1)} %get-tuple-element.46), channel_id=1, source_target_pairs={{0,1},{1,2},{2,3},{3,0},{4,5},{5,6},{6,7},{7,4},{8,9},{9,10},{10,1... | collective-permute-start | bytes 602120 | tf_op jit(solution)/shard_map/ppermute | solution.py:614
  16.5 1.5 %collective-permute-start.3 = (bf16[784,128]{1,0:T(8,128)(2,1)S(1)}, bf16[784,128]{1,0:T(8,128)(2,1)S(1)}, u32[]{:S(2)}, u32[]{:S(2)}) collective-permute-start(bf16[784,128]{1,0:T(8,128)(2,1)S(1)} %get-tuple-element.47), channel_id=1, source_target_pairs={{1,0},{2,1},{3,2},{0,3},{5,4},{6,5},{7,6},{4,7},{9,8},{10,9},{11,1... | collective-permute-start | bytes 602120 | tf_op jit(solution)/shard_map/ppermute | solution.py:615
  18.0 0.0 copy-done.1
  18.0 0.0 copy-done.3
  18.1 9.9 %shard_map.166 = (bf16[4,80,128]{2,1,0:T(8,128)(2,1)S(1)}, bf16[4,80,128]{2,1,0:T(8,128)(2,1)S(1)}, bf16[4,144,128]{2,1,0:T(8,128)(2,1)S(1)}, bf16[2,80,128]{2,1...) custom-call(bf16[64,4096]{1,0:T(8,128)(2,1)S(1)} %copy-done.2, ...), custom_call_target="tpu_custom_call" | custom-call | flops 1500000000 | bytes 1048576 | tf_op jit(solution)/shard_map/pallas_call | solution.py:48
  28.0 0.0 collective-permute-done.2.from_left.left
  28.0 0.0 collective-permute-done.3.from_right.right
  28.1 0.0 copy-start.6
  28.1 0.0 copy-start.8
  28.1 2.9 %shard_map.167 = (bf16[48,128]{1,0:T(8,128)(2,1)S(1)}, bf16[48,128]{1,0:T(8,128)(2,1)S(1)}, bf16[144,128]{1,0:T(8,128)(2,1)S(1)}, bf16[48,128]{1,0:T(8,128)(2,1)S(1)}) custom-call(s32[1]{0:T(128)} %bitcast.place, bf16[96,128]{1,0:T(8,128)(2,1)S(1)} %get-tuple-element.45.far_spec, bf16[784,128]{1,0:T(8,128)(2,1)S(1)} %collective-permute-done.2.from_left.left, ...), custom_call_target="tpu_custom_call" | custom-call | bytes 1048576 | tf_op jit(solution)/shard_map/pallas_call | solution.py:48
  30.9 1.5 %collective-permute-start.5 = (bf16[144,128]{1,0:T(8,128)(2,1)S(1)}, bf16[144,128]{1,0:T(8,128)(2,1)S(1)}, u32[]{:S(2)}, u32[]{:S(2)}) collective-permute-start(bf16[144,128]{1,0:T(8,128)(2,1)S(1)} %get-tuple-element.63), channel_id=1, source_target_pairs={{0,2},{1,3},{2,0},{3,1},{4,6},{5,7},{6,4},{7,5},{8,10},{9,11},{10,... | collective-permute-start | bytes 110600 | tf_op jit(solution)/shard_map/ppermute | solution.py:665
  32.4 2.1 %collective-permute-start.4 = (bf16[48,128]{1,0:T(8,128)(2,1)S(1)}, bf16[48,128]{1,0:T(8,128)(2,1)S(1)}, u32[]{:S(2)}, u32[]{:S(2)}) collective-permute-start(bf16[48,128]{1,0:T(8,128)(2,1)S(1)} %get-tuple-element.62), channel_id=1, source_target_pairs={{0,1},{1,2},{2,3},{3,0},{4,5},{5,6},{6,7},{7,4},{8,9},{9,10},{10,1... | collective-permute-start | bytes 36872 | tf_op jit(solution)/shard_map/ppermute | solution.py:666
  34.5 0.0 collective-permute-start.6
  34.5 1.6 %collective-permute-done.4.grad1 = bf16[48,128]{1,0:T(8,128)(2,1)S(1)} collective-permute-done((bf16[48,128]{1,0:T(8,128)(2,1)S(1)}, bf16[48,128]{1,0:T(8,128)(2,1)S(1)}, u32[]{:S(2)}, u32[]{:S(2)}) %collective-permute-start.4) | collective-permute-done | bytes 12320 | tf_op jit(solution)/shard_map/ppermute | solution.py:666
  36.1 3.3 %collective-permute-done.6.grad3 = bf16[48,128]{1,0:T(8,128)(2,1)S(1)} collective-permute-done((bf16[48,128]{1,0:T(8,128)(2,1)S(1)}, bf16[48,128]{1,0:T(8,128)(2,1)S(1)}, u32[]{:S(2)}, u32[]{:S(2)}) %collective-permute-start.6) | collective-permute-done | bytes 12320 | tf_op jit(solution)/shard_map/ppermute | solution.py:667
  39.4 0.0 collective-permute-done.5.grad2
  39.4 1.1 %shard_map.168 = f32[128,128]{1,0:T(8,128)} custom-call(s32[1]{0:T(128)} %bitcast.place, bf16[48,128]{1,0:T(8,128)(2,1)S(1)} %get-tuple-element.61.grad0, bf16[48,128]{1,0:T(8,128)(2,1)S(1)} %collective-permute-done.4.grad1, bf16[144,128]{1,0:T(8,128)(2,1)S(1)} %collective-permute-done.5.grad2, bf16[48,128]{1,0:T(8,128)(2,1)S(1)} %collective-permute-done.6.grad3, ...), custom_call_target="tpu_custom_call" | custom-call | bytes 1048576 | tf_op jit(solution)/shard_map/pallas_call | solution.py:48
  (8 shorter events, 0.0 us)
Async XLA Ops:
  1.7 9.5 %collective-permute-start.1 = (bf16[16,4096]{1,0:T(8,128)(2,1)S(1)}, bf16[16,4096]{1,0:T(8,128)(2,1)S(1)}, u32[]{:S(2)}, u32[]{:S(2)}) collective-permute-start(bf16[16,4096]{1,0:T(8,128)(2,1)S(1)} %get-tuple-element.44), channel_id=1, source_target_pairs={{4,0},{8,4},{12,8},{16,12},{20,16},{24,20},{28,24},{32,28},{36,32}... | collective-permute-start | bytes 393224 | tf_op jit(solution)/shard_map/ppermute | solution.py:557
  7.2 8.4 %collective-permute-start = (bf16[16,4096]{1,0:T(8,128)(2,1)S(1)}, bf16[16,4096]{1,0:T(8,128)(2,1)S(1)}, u32[]{:S(2)}, u32[]{:S(2)}) collective-permute-start(bf16[16,4096]{1,0:T(8,128)(2,1)S(1)} %get-tuple-element.36.packed), channel_id=1, source_target_pairs={{0,4},{4,8},{8,12},{12,16},{16,20},{20,24},{24,28},{28,32},{32,36}... | collective-permute-start | bytes 393224 | tf_op jit(solution)/shard_map/ppermute | solution.py:556
  9.2 8.9 %copy-start.1 = (bf16[128,4096]{1,0:T(8,128)(2,1)S(1)}, bf16[128,4096]{1,0:T(8,128)(2,1)}, u32[]{:S(2)}) copy-start(bf16[128,4096]{1,0:T(8,128)(2,1)} %a1.5) | copy-start | bytes 3145732
  9.2 8.9 %copy-start.2 = (bf16[64,4096]{1,0:T(8,128)(2,1)S(1)}, bf16[64,4096]{1,0:T(8,128)(2,1)}, u32[]{:S(2)}) copy-start(bf16[64,4096]{1,0:T(8,128)(2,1)} %a4.5) | copy-start | bytes 1572868
  9.2 8.8 %copy-start.3 = (bf16[64,4096]{1,0:T(8,128)(2,1)S(1)}, bf16[64,4096]{1,0:T(8,128)(2,1)}, u32[]{:S(2)}) copy-start(bf16[64,4096]{1,0:T(8,128)(2,1)} %a3.5) | copy-start | bytes 1572868
  9.2 8.8 %copy-start.4 = (bf16[64,2048]{1,0:T(8,128)(2,1)S(1)}, bf16[64,2048]{1,0:T(8,128)(2,1)}, u32[]{:S(2)}) copy-start(bf16[64,2048]{1,0:T(8,128)(2,1)} %t1.5) | copy-start | bytes 786436
  9.2 8.8 %copy-start.5 = (bf16[32,2048]{1,0:T(8,128)(2,1)S(1)}, bf16[32,2048]{1,0:T(8,128)(2,1)}, u32[]{:S(2)}) copy-start(bf16[32,2048]{1,0:T(8,128)(2,1)} %t2.5) | copy-start | bytes 393220
  9.2 8.8 %copy-start.7 = (f32[128,64]{0,1:T(8,128)S(1)}, f32[128,64]{0,1:T(8,128)}, u32[]{:S(2)}) copy-start(f32[128,64]{0,1:T(8,128)} %param.27) | copy-start | bytes 98308
  9.2 8.8 %copy-start.9 = (f32[64]{0:T(128)S(1)}, f32[64]{0:T(128)}, u32[]{:S(2)}) copy-start(f32[64]{0:T(128)} %param.28) | copy-start | bytes 772
  11.1 6.9 %copy-start = (bf16[128,4096]{1,0:T(8,128)(2,1)S(1)}, bf16[128,4096]{1,0:T(8,128)(2,1)}, u32[]{:S(2)}) copy-start(bf16[128,4096]{1,0:T(8,128)(2,1)} %a2.5) | copy-start | bytes 3145732
  15.9 12.1 %collective-permute-start.2 = (bf16[784,128]{1,0:T(8,128)(2,1)S(1)}, bf16[784,128]{1,0:T(8,128)(2,1)S(1)}, u32[]{:S(2)}, u32[]{:S(2)}) collective-permute-start(bf16[784,128]{1,0:T(8,128)(2,1)S(1)} %get-tuple-element.46), channel_id=1, source_target_pairs={{0,1},{1,2},{2,3},{3,0},{4,5},{5,6},{6,7},{7,4},{8,9},{9,10},{10,1... | collective-permute-start | bytes 602120 | tf_op jit(solution)/shard_map/ppermute | solution.py:614
  16.5 11.6 %collective-permute-start.3 = (bf16[784,128]{1,0:T(8,128)(2,1)S(1)}, bf16[784,128]{1,0:T(8,128)(2,1)S(1)}, u32[]{:S(2)}, u32[]{:S(2)}) collective-permute-start(bf16[784,128]{1,0:T(8,128)(2,1)S(1)} %get-tuple-element.47), channel_id=1, source_target_pairs={{1,0},{2,1},{3,2},{0,3},{5,4},{6,5},{7,6},{4,7},{9,8},{10,9},{11,1... | collective-permute-start | bytes 602120 | tf_op jit(solution)/shard_map/ppermute | solution.py:615
  28.1 11.4 %copy-start.6 = (bf16[1024,512]{1,0:T(8,128)(2,1)S(1)}, bf16[1024,512]{1,0:T(8,128)(2,1)}, u32[]{:S(2)}) copy-start(bf16[1024,512]{1,0:T(8,128)(2,1)} %constant.10.table) | copy-start | bytes 3145732
  28.1 11.4 %copy-start.8 = (f32[8,512]{1,0:T(8,128)S(1)}, f32[8,512]{1,0:T(8,128)}, u32[]{:S(2)}) copy-start(f32[8,512]{1,0:T(8,128)} %constant.9.clone.window) | copy-start | bytes 49156
  30.9 8.5 %collective-permute-start.5 = (bf16[144,128]{1,0:T(8,128)(2,1)S(1)}, bf16[144,128]{1,0:T(8,128)(2,1)S(1)}, u32[]{:S(2)}, u32[]{:S(2)}) collective-permute-start(bf16[144,128]{1,0:T(8,128)(2,1)S(1)} %get-tuple-element.63), channel_id=1, source_target_pairs={{0,2},{1,3},{2,0},{3,1},{4,6},{5,7},{6,4},{7,5},{8,10},{9,11},{10,... | collective-permute-start | bytes 110600 | tf_op jit(solution)/shard_map/ppermute | solution.py:665
  32.4 3.7 %collective-permute-start.4 = (bf16[48,128]{1,0:T(8,128)(2,1)S(1)}, bf16[48,128]{1,0:T(8,128)(2,1)S(1)}, u32[]{:S(2)}, u32[]{:S(2)}) collective-permute-start(bf16[48,128]{1,0:T(8,128)(2,1)S(1)} %get-tuple-element.62), channel_id=1, source_target_pairs={{0,1},{1,2},{2,3},{3,0},{4,5},{5,6},{6,7},{7,4},{8,9},{9,10},{10,1... | collective-permute-start | bytes 36872 | tf_op jit(solution)/shard_map/ppermute | solution.py:666
  34.5 4.9 %collective-permute-start.6 = (bf16[48,128]{1,0:T(8,128)(2,1)S(1)}, bf16[48,128]{1,0:T(8,128)(2,1)S(1)}, u32[]{:S(2)}, u32[]{:S(2)}) collective-permute-start(bf16[48,128]{1,0:T(8,128)(2,1)S(1)} %get-tuple-element.64), channel_id=1, source_target_pairs={{1,0},{2,1},{3,2},{0,3},{5,4},{6,5},{7,6},{4,7},{9,8},{10,9},{11,1... | collective-permute-start | bytes 36872 | tf_op jit(solution)/shard_map/ppermute | solution.py:667
